TPU v7x, 32 devices: a whole 2x2x4 slice. The times are simulated.
32 devices in a mesh: grp: 2 (over y), ja: 4 (over z), ia: 4 (over x, core).
Axes of the slice: x: 2, y: 2, z: 4, core: 2. Of those that a mesh axis runs over, the one named last changes fastest.
Arguments:
- pos_vel: float32 [6, 8192], P(None, ('grp', 'ja')), parts along dimension 1, may hold values from -6 to 6
- acc_jerk: float32 [6, 8192], P(None, ('grp', 'ja')), parts along dimension 1, may hold values from -6 to 6
- mass: float32 [8192], P(('grp', 'ja')), parts along dimension 0, may hold values from 7.324219e-05 to 0.0007324219
- age: float32 [8192], P(('grp', 'ja')), parts along dimension 0, may hold values from 0.125 to 0.5
- active_local: int32 [12288], P(('grp', 'ia')), parts along dimension 0, may hold values from 0 to 1023
- active_owner: int32 [12288], P(('grp', 'ia')), parts along dimension 0, may hold values from 0 to 3
Outputs:
- state: float32 [6, 12288], P(None, ('grp', 'ia')), parts along dimension 1
- forces: float32 [7, 12288], P(None, ('grp', 'ia')), parts along dimension 1
There are 2 independent parts, one for each index of `grp`. A program takes and returns all parts, laid end to end along the dimension named above; each array names one. Nothing has to cross between parts.
All inputs are finite; a program needn't handle non-finite values.
Results may differ from a plain program's by a relative error of at most 0.0003.
Values sent between devices are 32-bit elements; how exact they have to be, the bound alone decides.
No kernel may reach another device: no remote copies, remote signals or barrier semaphores. Data moves between devices by JAX's collectives and lax.ppermute only.
A program may use at most 64 MiB of HBM per device.

v0:
```python
import jax
import jax.numpy as jnp
from jax import lax
from jax.sharding import PartitionSpec as P

soften = 0.0004


def predict(pos_vel, acc_jerk, age):
    position = pos_vel[0:3]
    velocity = pos_vel[3:6]
    accel = acc_jerk[0:3]
    jolt = acc_jerk[3:6]
    step_len = age[None, :]
    new_pos = position + step_len * (velocity + step_len * (accel * 0.5 + step_len * jolt / 6.0))
    new_vel = velocity + step_len * (accel + step_len * jolt * 0.5)
    return jnp.concatenate([new_pos, new_vel], axis=0)


def pair_terms(targets, sources, masses):
    delta_pos = sources[0:3, :, None] - targets[0:3, None, :]
    delta_vel = sources[3:6, :, None] - targets[3:6, None, :]
    dist_sq = jnp.sum(delta_pos * delta_pos, axis=0) + soften
    inverse = lax.rsqrt(dist_sq)
    inv_sq = inverse * inverse
    weighted = masses[:, None] * inverse
    weighted_cube = weighted * inv_sq
    radial = 3.0 * jnp.sum(delta_pos * delta_vel, axis=0) * inv_sq
    accel = jnp.sum(weighted_cube[None] * delta_pos, axis=1)
    jolt = jnp.sum(weighted_cube[None] * (delta_vel - radial[None] * delta_pos), axis=1)
    potential = -jnp.sum(weighted, axis=0)
    return jnp.concatenate([accel, jolt, potential[None]], axis=0)


def block_terms(targets, sources, masses):
    count = targets.shape[1]
    width = min(512, count)
    nblocks = count // width
    src_count = sources.shape[1]
    src_width = min(512, src_count)
    src_blocks = src_count // src_width
    source_pieces = sources.reshape(6, src_blocks, src_width).transpose(1, 0, 2)
    mass_pieces = masses.reshape(src_blocks, src_width)
    pieces = targets.reshape(6, nblocks, width).transpose(1, 0, 2)

    def one_block(piece):

        def accumulate(total, parts):
            return (total + pair_terms(piece, parts[0], parts[1]), None)

        total, unused = lax.scan(
            accumulate, jnp.zeros((7, width), jnp.float32), (source_pieces, mass_pieces)
        )
        return total

    results = lax.map(one_block, pieces)
    return results.transpose(1, 0, 2).reshape(7, count)


def correct(history, forces):
    pred_pos = history[0:3]
    pred_vel = history[3:6]
    old_acc = history[6:9]
    old_jolt = history[9:12]
    step_len = history[12:13]
    new_acc = forces[0:3]
    new_jolt = forces[3:6]
    differ = old_acc - new_acc
    square = step_len * step_len
    cubed = square * step_len
    fourth = square * square
    fifth = fourth * step_len
    second = (-6.0 * differ - step_len * (4.0 * old_jolt + 2.0 * new_jolt)) / square
    third = (12.0 * differ + 6.0 * step_len * (old_jolt + new_jolt)) / cubed
    position = pred_pos + fourth / 24.0 * second + fifth / 120.0 * third
    velocity = pred_vel + cubed / 6.0 * second + fourth / 24.0 * third
    return jnp.concatenate([position, velocity], axis=0)


def local(pos_vel, acc_jerk, mass, age, active_local, active_owner):
    shard_rank = lax.axis_index("ja")
    predicted = predict(pos_vel, acc_jerk, age)
    stacked = jnp.concatenate([predicted, acc_jerk, age[None, :]], axis=0)
    picked = jnp.take(stacked, active_local, axis=1)
    owned = active_owner == shard_rank
    contrib = jnp.where(owned[None, :], picked, 0.0)
    history = lax.psum(contrib, "ja")
    partial_value = block_terms(history[0:6], predicted, mass)
    forces = lax.psum(partial_value, "ja")
    state = correct(history, forces)
    return (state, forces)


def solution(mesh):
    return jax.shard_map(
        local,
        mesh=mesh,
        in_specs=(
            P(None, ("grp", "ja")),
            P(None, ("grp", "ja")),
            P(("grp", "ja")),
            P(("grp", "ja")),
            P(("grp", "ia")),
            P(("grp", "ia")),
        ),
        out_specs=(P(None, ("grp", "ia")), P(None, ("grp", "ia"))),
        check_vma=False,
    )
```

profile of v0, /device:TPU:0, one launch (start us, length us, event | category | flops | bytes accessed | tf_op | source)
XLA Modules:
  0.0 92.8 jit_solution(16712219660879244907)
XLA Ops:
  7.2 0.0 all-reduce.2.cloned.1.call-start
  7.2 0.7 compare_select_fusion
  7.9 0.9 multiply_add_fusion.1
  8.8 0.8 pad_maximum_fusion
  9.6 0.0 copy-start.2
  9.6 0.0 copy-start.3
  9.6 0.2 copy.93
  9.8 0.0 copy-start.4
  9.9 2.6 %gather_fusion = f32[1536,13]{1,0:T(8,128)S(1)} fusion(f32[13,1024]{0,1:T(8,128)S(1)} %copy.93, s32[2048]{0:T(1024)S(1)} %pad_clamp_fusion), kind=kCustom, calls=%fused_computation | custom fusion | bytes 165888 | tf_op jit(solution)/shard_map/jit(_take)/gather | solution.py:84
  12.5 0.3 copy.94
  12.7 0.0 copy-done.2
  12.7 0.0 copy-done.3
  12.8 0.7 select_bitcast_fusion
  13.4 0.0 all-reduce.2.cloned.1.call-update
  13.4 0.0 copy-done.4
  13.5 37.3 %all-reduce.2.cloned.1.call-done = f32[13,1536]{1,0:T(8,128)} async-done(((f32[13,1536]{1,0:T(8,128)}), f32[13,1536]{1,0:T(8,128)}) %all-reduce.2.cloned.1.call-update) | async-done | bytes 79888 | tf_op jit(solution)/shard_map/psum | solution.py:87
  50.8 0.8 slice.71
  51.6 0.0 copy-start
  51.6 15.3 %while.22 = (s32[]{:T(128)}, f32[3,7,512]{2,1,0:T(8,128)S(1)}, f32[3,6,512]{2,1,0:T(8,128)S(1)}, f32[2,512]{1,0:T(2,128)S(1)}, f32[2,6,512]{2,1,0:T(8,128)S(1)},...) while((s32[]{:T(128)}, f32[3,7,512]{2,1,0:T(8,128)S(1)}, f32[3,6,512]{2,1,0:T(8,128)S(1)}, ...), condition=%wide.region_9.10_spmd, body=%wide.region_1.9_spmd.sunk | while | flops 12332038 | bytes 8612156 | solution.py:56
  51.6 5.1 %while.23 = (s32[]{:T(128)}, f32[7,512]{1,0:T(8,128)S(1)}, f32[2,512]{1,0:T(2,128)S(1)}, f32[2,6,512]{2,1,0:T(8,128)S(1)}, f32[6,512]{1,0:T(8,128)S(1)}, /*index=5*/s32[]{:T(128)}, s32[]{:T(128)}, s32[]{}) while((s32[]{:T(128)}, f32[7,512]{1,0:T(8,128)S(1)}, f32[2,512]{1,0:T(2,128)S(1)}, f32[2,6,512]{2,1,0:T(8,128)S(1)}, ...), condition=%wide.region_8.8_spmd.clone, body=%wide.region_2.7_spmd.clone.sunk | while | flops 12332036 | bytes 8554623 | solution.py:51
  51.7 1.0 %fusion.13 = (f32[512,512]{1,0:T(8,128)S(1)}, f32[512,512]{1,0:T(8,128)S(1)}) fusion(f32[3,512]{1,0:T(4,128)S(1)} %get-tuple-element.214, f32[3,512]{1,0:T(4,128)S(1)} %get-tuple-element.215, f32[3,512]{1,0:T(4,128)S(1)} %get-tuple-element.216, f32[3,512]{1,0:T(4,128)S(1)} %get-tuple-element.217), kind=kLoop, calls=%fused_computation.10.clone.1 | loop fusion | flops 4194304 | bytes 2121728 | tf_op jit(solution)/shard_map/while/body/eval_jaxpr/while/body/eval_jaxpr/reduce_sum | solution.py:28
  52.6 0.3 multiply_multiply_fusion.5
  53.0 1.1 %fusion.14 = (f32[3,512]{1,0:T(4,128)S(1)}, f32[3,512]{1,0:T(4,128)S(1)}) fusion(f32[512,512]{1,0:T(8,128)S(1)} %get-tuple-element.221, f32[3,512]{1,0:T(4,128)S(1)} %get-tuple-element.216, f32[3,512]{1,0:T(4,128)S(1)} %get-tuple-element.217, f32[512,512]{1,0:T(8,128)S(1)} %get-tuple-element.222, f32[3,512]{1,0:T(4,128)S(1)} %get-tuple-element.214, ...), kind=kLoop, calls=%fused_computation.9.clone.1 | loop fusion | flops 6288384 | bytes 2134016 | tf_op jit(solution)/shard_map/while/body/eval_jaxpr/while/body/eval_jaxpr/reduce_sum | solution.py:29
  54.2 1.0 %fusion.13 = (f32[512,512]{1,0:T(8,128)S(1)}, f32[512,512]{1,0:T(8,128)S(1)}) fusion(f32[3,512]{1,0:T(4,128)S(1)} %get-tuple-element.214, f32[3,512]{1,0:T(4,128)S(1)} %get-tuple-element.215, f32[3,512]{1,0:T(4,128)S(1)} %get-tuple-element.216, f32[3,512]{1,0:T(4,128)S(1)} %get-tuple-element.217), kind=kLoop, calls=%fused_computation.10.clone.1 | loop fusion | flops 4194304 | bytes 2121728 | tf_op jit(solution)/shard_map/while/body/eval_jaxpr/while/body/eval_jaxpr/reduce_sum | solution.py:28
  55.2 0.3 multiply_multiply_fusion.5
  55.5 1.1 %fusion.14 = (f32[3,512]{1,0:T(4,128)S(1)}, f32[3,512]{1,0:T(4,128)S(1)}) fusion(f32[512,512]{1,0:T(8,128)S(1)} %get-tuple-element.221, f32[3,512]{1,0:T(4,128)S(1)} %get-tuple-element.216, f32[3,512]{1,0:T(4,128)S(1)} %get-tuple-element.217, f32[512,512]{1,0:T(8,128)S(1)} %get-tuple-element.222, f32[3,512]{1,0:T(4,128)S(1)} %get-tuple-element.214, ...), kind=kLoop, calls=%fused_computation.9.clone.1 | loop fusion | flops 6288384 | bytes 2134016 | tf_op jit(solution)/shard_map/while/body/eval_jaxpr/while/body/eval_jaxpr/reduce_sum | solution.py:29
  56.7 5.1 %while.23 = (s32[]{:T(128)}, f32[7,512]{1,0:T(8,128)S(1)}, f32[2,512]{1,0:T(2,128)S(1)}, f32[2,6,512]{2,1,0:T(8,128)S(1)}, f32[6,512]{1,0:T(8,128)S(1)}, /*index=5*/s32[]{:T(128)}, s32[]{:T(128)}, s32[]{}) while((s32[]{:T(128)}, f32[7,512]{1,0:T(8,128)S(1)}, f32[2,512]{1,0:T(2,128)S(1)}, f32[2,6,512]{2,1,0:T(8,128)S(1)}, ...), condition=%wide.region_8.8_spmd.clone, body=%wide.region_2.7_spmd.clone.sunk | while | flops 12332036 | bytes 8554623 | solution.py:51
  56.8 1.0 %fusion.13 = (f32[512,512]{1,0:T(8,128)S(1)}, f32[512,512]{1,0:T(8,128)S(1)}) fusion(f32[3,512]{1,0:T(4,128)S(1)} %get-tuple-element.214, f32[3,512]{1,0:T(4,128)S(1)} %get-tuple-element.215, f32[3,512]{1,0:T(4,128)S(1)} %get-tuple-element.216, f32[3,512]{1,0:T(4,128)S(1)} %get-tuple-element.217), kind=kLoop, calls=%fused_computation.10.clone.1 | loop fusion | flops 4194304 | bytes 2121728 | tf_op jit(solution)/shard_map/while/body/eval_jaxpr/while/body/eval_jaxpr/reduce_sum | solution.py:28
  57.8 0.3 multiply_multiply_fusion.5
  58.1 1.1 %fusion.14 = (f32[3,512]{1,0:T(4,128)S(1)}, f32[3,512]{1,0:T(4,128)S(1)}) fusion(f32[512,512]{1,0:T(8,128)S(1)} %get-tuple-element.221, f32[3,512]{1,0:T(4,128)S(1)} %get-tuple-element.216, f32[3,512]{1,0:T(4,128)S(1)} %get-tuple-element.217, f32[512,512]{1,0:T(8,128)S(1)} %get-tuple-element.222, f32[3,512]{1,0:T(4,128)S(1)} %get-tuple-element.214, ...), kind=kLoop, calls=%fused_computation.9.clone.1 | loop fusion | flops 6288384 | bytes 2134016 | tf_op jit(solution)/shard_map/while/body/eval_jaxpr/while/body/eval_jaxpr/reduce_sum | solution.py:29
  59.3 1.0 %fusion.13 = (f32[512,512]{1,0:T(8,128)S(1)}, f32[512,512]{1,0:T(8,128)S(1)}) fusion(f32[3,512]{1,0:T(4,128)S(1)} %get-tuple-element.214, f32[3,512]{1,0:T(4,128)S(1)} %get-tuple-element.215, f32[3,512]{1,0:T(4,128)S(1)} %get-tuple-element.216, f32[3,512]{1,0:T(4,128)S(1)} %get-tuple-element.217), kind=kLoop, calls=%fused_computation.10.clone.1 | loop fusion | flops 4194304 | bytes 2121728 | tf_op jit(solution)/shard_map/while/body/eval_jaxpr/while/body/eval_jaxpr/reduce_sum | solution.py:28
  60.3 0.3 multiply_multiply_fusion.5
  60.6 1.1 %fusion.14 = (f32[3,512]{1,0:T(4,128)S(1)}, f32[3,512]{1,0:T(4,128)S(1)}) fusion(f32[512,512]{1,0:T(8,128)S(1)} %get-tuple-element.221, f32[3,512]{1,0:T(4,128)S(1)} %get-tuple-element.216, f32[3,512]{1,0:T(4,128)S(1)} %get-tuple-element.217, f32[512,512]{1,0:T(8,128)S(1)} %get-tuple-element.222, f32[3,512]{1,0:T(4,128)S(1)} %get-tuple-element.214, ...), kind=kLoop, calls=%fused_computation.9.clone.1 | loop fusion | flops 6288384 | bytes 2134016 | tf_op jit(solution)/shard_map/while/body/eval_jaxpr/while/body/eval_jaxpr/reduce_sum | solution.py:29
  61.8 5.1 %while.23 = (s32[]{:T(128)}, f32[7,512]{1,0:T(8,128)S(1)}, f32[2,512]{1,0:T(2,128)S(1)}, f32[2,6,512]{2,1,0:T(8,128)S(1)}, f32[6,512]{1,0:T(8,128)S(1)}, /*index=5*/s32[]{:T(128)}, s32[]{:T(128)}, s32[]{}) while((s32[]{:T(128)}, f32[7,512]{1,0:T(8,128)S(1)}, f32[2,512]{1,0:T(2,128)S(1)}, f32[2,6,512]{2,1,0:T(8,128)S(1)}, ...), condition=%wide.region_8.8_spmd.clone, body=%wide.region_2.7_spmd.clone.sunk | while | flops 12332036 | bytes 8554623 | solution.py:51
  61.9 1.0 %fusion.13 = (f32[512,512]{1,0:T(8,128)S(1)}, f32[512,512]{1,0:T(8,128)S(1)}) fusion(f32[3,512]{1,0:T(4,128)S(1)} %get-tuple-element.214, f32[3,512]{1,0:T(4,128)S(1)} %get-tuple-element.215, f32[3,512]{1,0:T(4,128)S(1)} %get-tuple-element.216, f32[3,512]{1,0:T(4,128)S(1)} %get-tuple-element.217), kind=kLoop, calls=%fused_computation.10.clone.1 | loop fusion | flops 4194304 | bytes 2121728 | tf_op jit(solution)/shard_map/while/body/eval_jaxpr/while/body/eval_jaxpr/reduce_sum | solution.py:28
  62.9 0.3 multiply_multiply_fusion.5
  63.2 1.1 %fusion.14 = (f32[3,512]{1,0:T(4,128)S(1)}, f32[3,512]{1,0:T(4,128)S(1)}) fusion(f32[512,512]{1,0:T(8,128)S(1)} %get-tuple-element.221, f32[3,512]{1,0:T(4,128)S(1)} %get-tuple-element.216, f32[3,512]{1,0:T(4,128)S(1)} %get-tuple-element.217, f32[512,512]{1,0:T(8,128)S(1)} %get-tuple-element.222, f32[3,512]{1,0:T(4,128)S(1)} %get-tuple-element.214, ...), kind=kLoop, calls=%fused_computation.9.clone.1 | loop fusion | flops 6288384 | bytes 2134016 | tf_op jit(solution)/shard_map/while/body/eval_jaxpr/while/body/eval_jaxpr/reduce_sum | solution.py:29
  64.4 1.0 %fusion.13 = (f32[512,512]{1,0:T(8,128)S(1)}, f32[512,512]{1,0:T(8,128)S(1)}) fusion(f32[3,512]{1,0:T(4,128)S(1)} %get-tuple-element.214, f32[3,512]{1,0:T(4,128)S(1)} %get-tuple-element.215, f32[3,512]{1,0:T(4,128)S(1)} %get-tuple-element.216, f32[3,512]{1,0:T(4,128)S(1)} %get-tuple-element.217), kind=kLoop, calls=%fused_computation.10.clone.1 | loop fusion | flops 4194304 | bytes 2121728 | tf_op jit(solution)/shard_map/while/body/eval_jaxpr/while/body/eval_jaxpr/reduce_sum | solution.py:28
  65.4 0.3 multiply_multiply_fusion.5
  65.7 1.1 %fusion.14 = (f32[3,512]{1,0:T(4,128)S(1)}, f32[3,512]{1,0:T(4,128)S(1)}) fusion(f32[512,512]{1,0:T(8,128)S(1)} %get-tuple-element.221, f32[3,512]{1,0:T(4,128)S(1)} %get-tuple-element.216, f32[3,512]{1,0:T(4,128)S(1)} %get-tuple-element.217, f32[512,512]{1,0:T(8,128)S(1)} %get-tuple-element.222, f32[3,512]{1,0:T(4,128)S(1)} %get-tuple-element.214, ...), kind=kLoop, calls=%fused_computation.9.clone.1 | loop fusion | flops 6288384 | bytes 2134016 | tf_op jit(solution)/shard_map/while/body/eval_jaxpr/while/body/eval_jaxpr/reduce_sum | solution.py:29
  66.9 18.2 %psum.15 = f32[7,1536]{1,0:T(8,128)S(1)} all-reduce(f32[7,1536]{1,0:T(8,128)S(1)} %bitcast.36), channel_id=1, replica_groups=mesh['grp'=2,'ja'=4,'ia'=4] {'ja'}, use_global_device_ids=true, to_apply=%region_10.11 | all-reduce | flops 10752 | bytes 86016 | tf_op jit(solution)/shard_map/psum | solution.py:89
  85.1 0.0 copy-done
  85.1 0.0 copy-start.1
  85.1 0.1 multiply_reduce_fusion.3
  85.2 0.1 fusion.6
  85.3 0.6 pad_maximum_fusion.1
  86.0 0.0 copy-done.1
  (45 shorter events, 0.4 us)
Async XLA Ops:
  7.2 43.6 %all-reduce.2.cloned.1.call-start = ((), (), s32[]{:S(2)}) async-start(), calls=%async_computation | async-start | bytes 196608 | tf_op jit(solution)/shard_map/psum | solution.py:87
  9.6 3.1 %copy-start.2 = (s32[1536]{0:T(1024)S(1)}, s32[1536]{0:T(1024)}, u32[]{:S(2)}) copy-start(s32[1536]{0:T(1024)} %param.14) | copy-start | bytes 18436
  9.6 3.1 %copy-start.3 = (s32[1536]{0:T(1024)S(1)}, s32[1536]{0:T(1024)}, u32[]{:S(2)}) copy-start(s32[1536]{0:T(1024)} %param.15) | copy-start | bytes 18436
  9.8 3.6 %copy-start.4 = (f32[1024]{0:T(1024)S(1)}, f32[1024]{0:T(1024)}, u32[]{:S(2)}) copy-start(f32[1024]{0:T(1024)} %param.12) | copy-start | bytes 12292
  51.6 33.5 %copy-start = (f32[13,1536]{1,0:T(8,128)S(1)}, f32[13,1536]{1,0:T(8,128)}, u32[]{:S(2)}) copy-start(f32[13,1536]{1,0:T(8,128)} %all-reduce.2.cloned.1.call-done) | copy-start | bytes 239620
  85.1 0.9 copy-start.1
Sparse Core Ops, SparseCore 0:
  13.5 37.1 all-reduce.1
where the time goes:
time: 93.2 us; the launch traced here: 92.8 us
  waiting for transfers between devices  37.3 us (40%)
  other arithmetic  18.4 us (20%)
  blocking collectives  18.2 us (20%)
  between operations  14.2 us (15%)
  local copies, waits for them, and re-layouts  4.12 us (4%)
    psum x1, waiting for transfers between devices, local(): history = lax.psum(contrib, 'ja')  37.3 us
    psum x1, blocking collectives, local(): forces = lax.psum(partial_value, 'ja')  18.2 us
    reduce_sum x6, other arithmetic, pair_terms(): accel = jnp.sum(weighted_cube[None] * delta_pos, axis=1)  6.74 us
    reduce_sum x6, other arithmetic, pair_terms(): radial = 3.0 * jnp.sum(delta_pos * delta_vel, axis=0) * inv_sq  5.85 us
    gather x2, local copies, waits for them, and re-layouts, local(): picked = jnp.take(stacked, active_local, axis=1)  2.86 us
  transfers between devices with their start and end apart: 1, of which 1 were waited for; matrix products, arithmetic and copies ran while one was open for 0% of the time, Pallas kernels for 0%

commit v1 on v0

--- a/solution.py
+++ b/solution.py
@@ -1,9 +1,18 @@
 import jax
 import jax.numpy as jnp
 from jax import lax
+from jax.experimental import pallas as pl
+from jax.experimental.pallas import tpu as pltpu
 from jax.sharding import PartitionSpec as P
 
 soften = 0.0004
+f32 = jnp.float32
+bf16 = jnp.bfloat16
+LANES = 128
+ROWS = 16
+COLS = 64
+VMEM = pl.BlockSpec(memory_space=pltpu.VMEM)
+BOTH_MINOR = (((1,), (1,)), ((), ()))
 
 
 def predict(pos_vel, acc_jerk, age):
@@ -57,14 +66,7 @@
     return results.transpose(1, 0, 2).reshape(7, count)
 
 
-def correct(history, forces):
-    pred_pos = history[0:3]
-    pred_vel = history[3:6]
-    old_acc = history[6:9]
-    old_jolt = history[9:12]
-    step_len = history[12:13]
-    new_acc = forces[0:3]
-    new_jolt = forces[3:6]
+def correct(pred_pos, pred_vel, old_acc, old_jolt, step_len, new_acc, new_jolt):
     differ = old_acc - new_acc
     square = step_len * step_len
     cubed = square * step_len
@@ -74,10 +76,10 @@
     third = (12.0 * differ + 6.0 * step_len * (old_jolt + new_jolt)) / cubed
     position = pred_pos + fourth / 24.0 * second + fifth / 120.0 * third
     velocity = pred_vel + cubed / 6.0 * second + fourth / 24.0 * third
-    return jnp.concatenate([position, velocity], axis=0)
-
-
-def local(pos_vel, acc_jerk, mass, age, active_local, active_owner):
+    return position, velocity
+
+
+def general(pos_vel, acc_jerk, mass, age, active_local, active_owner):
     shard_rank = lax.axis_index("ja")
     predicted = predict(pos_vel, acc_jerk, age)
     stacked = jnp.concatenate([predicted, acc_jerk, age[None, :]], axis=0)
@@ -87,11 +89,291 @@
     history = lax.psum(contrib, "ja")
     partial_value = block_terms(history[0:6], predicted, mass)
     forces = lax.psum(partial_value, "ja")
-    state = correct(history, forces)
-    return (state, forces)
+    position, velocity = correct(
+        history[0:3], history[3:6], history[6:9], history[9:12], history[12:13], forces[0:3], forces[3:6]
+    )
+    return (jnp.concatenate([position, velocity], axis=0), forces)
+
+
+def predict_kernel(pv_ref, aj_ref, mass_ref, age_ref, src_ref, own_ref):
+    width = own_ref.shape[1]
+    step_len = age_ref[...]
+    accel = aj_ref[0:3, :]
+    jolt = aj_ref[3:6, :]
+    velocity = pv_ref[3:6, :]
+    src_ref[0:3, :] = pv_ref[0:3, :] + step_len * (velocity + step_len * (accel * 0.5 + step_len * jolt / 6.0))
+    src_ref[3:6, :] = velocity + step_len * (accel + step_len * jolt * 0.5)
+    src_ref[6:7, :] = mass_ref[...]
+    src_ref[7:8, :] = step_len
+    mine = pl.ds(pl.multiple_of(lax.axis_index("ia") * width, LANES), width)
+    own_ref[0:6, :] = src_ref[0:6, mine]
+    own_ref[6:12, :] = aj_ref[:, mine]
+    own_ref[12:13, :] = age_ref[:, mine]
+    own_ref[13:16, :] = jnp.zeros((3, width), f32)
+
+
+def three_parts(x):
+    high = x.astype(bf16).astype(f32)
+    rest = x - high
+    mid = rest.astype(bf16).astype(f32)
+    return high, mid, rest - mid
+
+
+def spread_targets(own_ref, wide):
+    width = own_ref.shape[1]
+    turned = jnp.transpose(own_ref[0:8, :])
+    for c in range(6):
+        wide[c] = jnp.broadcast_to(turned[:, c : c + 1], (width, LANES))
+
+
+def clear_features(feat):
+    count = feat.shape[2]
+    feat[...] = jnp.zeros(feat.shape, f32)
+    one = jnp.ones((1, count), f32)
+    feat[0, 18:19, :] = one
+    feat[1, 41:42, :] = one
+
+
+def source_features(source, feat, right, width):
+    rows = 0
+    for x in (*three_parts(source[0:3, :]), *three_parts(source[3:6, :])):
+        feat[0, rows : rows + 3, :] = x
+        if rows < 9:
+            feat[1, 32 + rows : 35 + rows, :] = x
+        rows += 3
+    for k in range(right.shape[0]):
+        for i in range(4):
+            right[k, :, i * width : i * width + width] = feat[i // 2, :, k * width : k * width + width].astype(bf16)
+
+
+def pair_chunk(source, offset, wide, left, pot_ref, diagonal):
+    width = wide.shape[1]
+    for rb in range(width // ROWS):
+        rs = slice(rb * ROWS, rb * ROWS + ROWS)
+        target = [wide[c, rs, :] for c in range(6)]
+        pot = pot_ref[rs, :]
+        for j in range(width // LANES):
+            cs = pl.ds(offset + LANES * j, LANES)
+            row = [jnp.broadcast_to(source[c : c + 1, cs], (ROWS, LANES)) for c in range(7)]
+            dx, dy, dz = (row[c] - target[c] for c in range(3))
+            ex, ey, ez = (row[c] - target[c] for c in range(3, 6))
+            inverse = lax.rsqrt(((dx * dx + soften) + dy * dy) + dz * dz)
+            inv_sq = inverse * inverse
+            weighted = row[6] * inverse
+            pot = pot + weighted
+            cube = weighted * inv_sq
+            if diagonal and rb * ROWS // LANES == j:
+                here = lax.broadcasted_iota(jnp.int32, (ROWS, LANES), 0) + (rb * ROWS - j * LANES)
+                there = lax.broadcasted_iota(jnp.int32, (ROWS, LANES), 1)
+                cube = jnp.where(here == there, 0.0, cube)
+            radial = cube * ((dx * ex + dy * ey + dz * ez) * inv_sq)
+            parts = (
+                cube,
+                cube - cube.astype(bf16).astype(f32),
+                radial,
+                radial - radial.astype(bf16).astype(f32),
+            )
+            for i, x in enumerate(parts):
+                left[rs, i * width + LANES * j : i * width + LANES * j + LANES] = x
+        pot_ref[rs, :] = pot
+
+
+def add_chunk(left, right, sum_ref):
+    sum_ref[...] += lax.dot_general(left[...].astype(bf16), right, BOTH_MINOR, preferred_element_type=f32)
+
+
+def local_kernel(src_ref, own_ref, sum_ref, pot_ref, feat, right, wide, left):
+    width = own_ref.shape[1]
+    chunks = right.shape[0]
+    spread_targets(own_ref, wide)
+    clear_features(feat)
+    source_features(src_ref, feat, right, width)
+    sum_ref[...] = jnp.zeros(sum_ref.shape, f32)
+    pot_ref[...] = jnp.zeros(pot_ref.shape, f32)
+    first = lax.axis_index("ia")
+    turn = [lax.rem(first + k, chunks) for k in range(chunks)]
+    for k in range(chunks):
+        pair_chunk(src_ref, pl.multiple_of(turn[k] * width, LANES), wide, left.at[k % 2], pot_ref, k == 0)
+        if k:
+            add_chunk(left.at[(k - 1) % 2], right[turn[k - 1]], sum_ref)
+    add_chunk(left.at[(chunks - 1) % 2], right[turn[chunks - 1]], sum_ref)
+
+
+def remote_kernel(*refs):
+    count = len(refs) - 8
+    sources = refs[:count]
+    own_ref, sum_in, pot_in, out_ref, feat, right, wide, left = refs[count:]
+    pl.run_scoped(
+        lambda sum_ref, pot_ref: remote_body(
+            sources, own_ref, sum_in, pot_in, out_ref, feat, right, wide, left, sum_ref, pot_ref
+        ),
+        pltpu.VMEM(sum_in.shape, f32),
+        pltpu.VMEM(pot_in.shape, f32),
+    )
+
+
+def remote_body(sources, own_ref, sum_in, pot_in, out_ref, feat, right, wide, left, sum_ref, pot_ref):
+    width = own_ref.shape[1]
+    chunks = right.shape[0]
+    spread_targets(own_ref, wide)
+    clear_features(feat)
+    sum_ref[...] = sum_in[...]
+    pot_ref[...] = pot_in[...]
+    for source in sources:
+        source_features(source, feat, right, width)
+        pair_chunk(source, 0, wide, left.at[0], pot_ref, False)
+
+        def two(i, unused):
+            pair_chunk(source, pl.multiple_of((2 * i + 1) * width, LANES), wide, left.at[1], pot_ref, False)
+            add_chunk(left.at[0], right[2 * i], sum_ref)
+            pair_chunk(source, pl.multiple_of((2 * i + 2) * width, LANES), wide, left.at[0], pot_ref, False)
+            add_chunk(left.at[1], right[2 * i + 1], sum_ref)
+            return 0
+
+        lax.fori_loop(0, (chunks - 2) // 2, two, 0)
+        pair_chunk(source, (chunks - 1) * width, wide, left.at[1], pot_ref, False)
+        add_chunk(left.at[0], right[chunks - 2], sum_ref)
+        add_chunk(left.at[1], right[chunks - 1], sum_ref)
+    sums = jnp.transpose(sum_ref[...])
+    pot = jnp.sum(jnp.transpose(pot_ref[...]), axis=0, keepdims=True)
+    pos = own_ref[0:3, :]
+    vel = own_ref[3:6, :]
+    total = sums[18:19, :]
+    new_acc = (sums[0:3, :] - pos * total) + sums[3:6, :] + sums[6:9, :]
+    flow = (sums[9:12, :] - vel * total) + sums[12:15, :] + sums[15:18, :]
+    pull = (sums[32:35, :] - pos * sums[41:42, :]) + sums[35:38, :] + sums[38:41, :]
+    new_jolt = flow - 3.0 * pull
+    position, velocity = correct(
+        pos, vel, own_ref[6:9, :], own_ref[9:12, :], own_ref[12:13, :], new_acc, new_jolt
+    )
+    out_ref[0:3, :] = position
+    out_ref[3:6, :] = velocity
+    out_ref[6:8, :] = jnp.zeros((2, width), f32)
+    out_ref[8:11, :] = new_acc
+    out_ref[11:14, :] = new_jolt
+    out_ref[14:15, :] = -pot
+    out_ref[15:16, :] = jnp.zeros((1, width), f32)
+
+
+def pick_kernel(ia_bits, ja_bits, width, table_ref, local_ref, owner_ref, state_ref, forces_ref):
+    count = local_ref.shape[1]
+    per = width // LANES
+    my_ja = lax.axis_index("ja")
+    my_ia = lax.axis_index("ia")
+    for b in range(count // LANES):
+        cs = slice(b * LANES, b * LANES + LANES)
+        local = local_ref[:, cs]
+        apart_ja = lax.bitwise_xor(owner_ref[:, cs], my_ja)
+        apart_ia = lax.bitwise_xor(local // width, my_ia)
+        parity = apart_ia
+        for i in range(1, ia_bits):
+            parity = lax.bitwise_xor(parity, lax.shift_right_logical(apart_ia, i))
+        flips = parity
+        for i in range(ja_bits):
+            flips = lax.bitwise_xor(flips, lax.shift_right_logical(apart_ja, i))
+        slot = apart_ja + lax.shift_left(lax.shift_right_logical(apart_ia, 1), ja_bits)
+        slot = slot + lax.shift_left(lax.bitwise_and(flips, 1), ja_bits + ia_bits - 1)
+        within = lax.rem(local, width)
+        piece = jnp.broadcast_to(slot * per + within // LANES, (8, LANES))
+        lane = jnp.broadcast_to(lax.rem(within, LANES), (8, LANES))
+        state = jnp.zeros((8, LANES), f32)
+        forces = jnp.zeros((8, LANES), f32)
+        for t in range(table_ref.shape[1] // LANES):
+            hit = piece == t
+            ts = slice(t * LANES, t * LANES + LANES)
+            state = jnp.where(hit, jnp.take_along_axis(table_ref[0:8, ts], lane, axis=1), state)
+            forces = jnp.where(hit, jnp.take_along_axis(table_ref[8:16, ts], lane, axis=1), forces)
+        state_ref[:, cs] = state[0:6, :]
+        forces_ref[:, cs] = forces[0:7, :]
+
+
+def shape_of(*dims):
+    return jax.ShapeDtypeStruct(dims, f32)
+
+
+def all_stars(nj, ni, pos_vel, acc_jerk, mass, age, active_local, active_owner):
+    stars = mass.shape[0]
+    width = stars // ni
+    chunks = stars // width
+    ja_bits = nj.bit_length() - 1
+    ia_bits = ni.bit_length() - 1
+
+    def exchange(x, dj, di):
+        pairs = [(j * ni + i, (j ^ dj) * ni + (i ^ di)) for j in range(nj) for i in range(ni)]
+        return lax.ppermute(x, ("ja", "ia"), pairs)
+
+    src, own = pl.pallas_call(
+        predict_kernel,
+        out_shape=(shape_of(8, stars), shape_of(16, width)),
+        in_specs=[VMEM] * 4,
+        out_specs=(VMEM, VMEM),
+        name="predict",
+    )(pos_vel, acc_jerk, mass[None, :], age[None, :])
+    others = [exchange(src, d, 1) for d in range(1, nj)]
+    scratch = [
+        pltpu.VMEM((2, COLS, stars), f32),
+        pltpu.VMEM((chunks, COLS, 4 * width), bf16),
+        pltpu.VMEM((6, width, LANES), f32),
+        pltpu.VMEM((2, width, 4 * width), f32),
+    ]
+    pairs_cost = pl.CostEstimate(flops=40 * width * stars, transcendentals=width * stars, bytes_accessed=400000)
+    sums, pot = pl.pallas_call(
+        local_kernel,
+        out_shape=(shape_of(width, COLS), shape_of(width, LANES)),
+        in_specs=[VMEM] * 2,
+        out_specs=(VMEM, VMEM),
+        scratch_shapes=scratch,
+        cost_estimate=pairs_cost,
+        name="near",
+    )(src, own)
+    block = pl.pallas_call(
+        remote_kernel,
+        out_shape=shape_of(16, width),
+        in_specs=[VMEM] * (len(others) + 3),
+        out_specs=VMEM,
+        scratch_shapes=scratch,
+        name="far",
+    )(*others, own, sums, pot)
+    for bit in range(ja_bits):
+        block = jnp.concatenate([block, exchange(block, 1 << bit, 1)], axis=1)
+    for bit in range(1, ia_bits):
+        block = jnp.concatenate([block, exchange(block, 0, (1 << bit) + 1)], axis=1)
+    block = jnp.concatenate([block, exchange(block, 0, 1)], axis=1)
+    count = active_local.shape[0]
+
+    def pick(*refs):
+        pick_kernel(ia_bits, ja_bits, width, *refs)
+
+    return pl.pallas_call(
+        pick,
+        out_shape=(shape_of(6, count), shape_of(7, count)),
+        in_specs=[VMEM] * 3,
+        out_specs=(VMEM, VMEM),
+        name="pick",
+    )(block, active_local[None, :], active_owner[None, :])
 
 
 def solution(mesh):
+    nj = mesh.shape["ja"]
+    ni = mesh.shape["ia"]
+
+    def local(pos_vel, acc_jerk, mass, age, active_local, active_owner):
+        stars = mass.shape[0]
+        width = stars // ni
+        fits = (
+            nj & (nj - 1) == 0
+            and ni & (ni - 1) == 0
+            and nj > 1
+            and ni > 1
+            and stars % ni == 0
+            and width % LANES == 0
+            and width <= 256
+            and active_local.shape[0] % LANES == 0
+            and stars * nj <= active_local.shape[0] * ni
+        )
+        args = (pos_vel, acc_jerk, mass, age, active_local, active_owner)
+        return all_stars(nj, ni, *args) if fits else general(*args)
+
     return jax.shard_map(
         local,
         mesh=mesh,

time: 93.2 us -> 36.5 us (0.39)
  waiting for transfers between devices: 37.3 us -> 13.6 us
  other arithmetic: 18.4 us -> 0.02 us
  blocking collectives: 18.2 us -> 0 us
  between operations: 14.2 us -> 0.7 us
  Pallas kernels: 0 us -> 12.6 us
  starting transfers between devices: 0.04 us -> 6.76 us
  local copies, waits for them, and re-layouts: 4.12 us -> 2.54 us
    psum x1 -> x0, waiting for transfers between devices: 37.3 us -> none  [local(): history = lax.psum(contrib, 'ja')]
    psum x1 -> x0, blocking collectives: 18.2 us -> none  [local(): forces = lax.psum(partial_value, 'ja')]
    ppermute x0 -> x7, waiting for transfers between devices: none -> 13.6 us  [exchange(): return lax.ppermute(x, ('ja', 'ia'), pairs)]
    reduce_sum x12 -> x0, other arithmetic: 12.6 us -> none  [the longest x6 6.74 us: pair_terms(): accel = jnp.sum(weighted_cube[None] * delta_pos, axis=1)]
    pallas_call x0 -> x4, Pallas kernels: none -> 12.6 us  [the longest x1 5.57 us: all_stars(): pl.pallas_call(remote_kernel, out_shape=shape_of(16, width), in_specs=[VM...]
    ppermute x0 -> x7, starting transfers between devices: none -> 6.76 us  [exchange(): return lax.ppermute(x, ('ja', 'ia'), pairs)]
    gather x2 -> x0, local copies, waits for them, and re-layouts: 2.86 us -> none  [local(): picked = jnp.take(stacked, active_local, axis=1)]
    mul x6 -> x0, other arithmetic: 1.86 us -> none  [pair_terms(): weighted_cube = weighted * inv_sq]
  transfers between devices with their start and end apart: 1 -> 7, of which waited for: 1 -> 5; matrix products, arithmetic and copies ran while one was open for 0% -> 3% of each run, Pallas kernels for 0% -> 8%
where the time goes in v1:
time: 36.5 us; the launch traced here: 36.2 us
  waiting for transfers between devices  13.6 us (37%)
  Pallas kernels  12.6 us (35%)
  starting transfers between devices  6.76 us (19%)
  local copies, waits for them, and re-layouts  2.54 us (7%)
  between operations  0.7 us (2%)
    ppermute x7, waiting for transfers between devices, exchange(): return lax.ppermute(x, ('ja', 'ia'), pairs)  13.6 us
    ppermute x7, starting transfers between devices, exchange(): return lax.ppermute(x, ('ja', 'ia'), pairs)  6.76 us
    pallas_call x1, Pallas kernels, all_stars(): pl.pallas_call(remote_kernel, out_shape=shape_of(16, width), in_specs=[VM...  5.57 us
    pallas_call x1, Pallas kernels, all_stars(): pl.pallas_call(local_kernel, out_shape=(shape_of(width, COLS), shape_of(w...  3.06 us
    pallas_call x1, Pallas kernels, all_stars(): pl.pallas_call(pick, out_shape=(shape_of(6, count), shape_of(7, count)),...  2.51 us
    pallas_call x1, Pallas kernels, all_stars(): pl.pallas_call(predict_kernel, out_shape=(shape_of(8, stars), shape_of(16...  1.42 us
    unnamed x18, local copies, waits for them, and re-layouts  1.33 us
  transfers between devices with their start and end apart: 7, of which 5 were waited for; matrix products, arithmetic and copies ran while one was open for 3% of the time, Pallas kernels for 8%

profile of v1, /device:TPU:0, one launch (start us, length us, event | category | flops | bytes accessed | tf_op | source)
XLA Modules:
  0.0 36.2 jit_solution(13807600908161826351)
XLA Ops:
  0.6 1.4 %predict.1 = (f32[8,1024]{1,0:T(8,128)}, f32[16,256]{1,0:T(8,128)}) custom-call(f32[6,1024]{1,0:T(8,128)} %pv_ref.1, f32[6,1024]{1,0:T(8,128)} %aj_ref.1, f32[1,1024]{1,0:T(1,128)} %bitcast.2, f32[1,1024]{1,0:T(1,128)} %bitcast.3), custom_call_target="tpu_custom_call" | custom-call | tf_op jit(solution)/shard_map/predict/pallas_call | solution.py:305
  2.1 2.5 %collective-permute-start = (f32[8,1024]{1,0:T(8,128)}, f32[8,1024]{1,0:T(8,128)S(1)}, u32[]{:S(2)}, u32[]{:S(2)}) collective-permute-start(f32[8,1024]{1,0:T(8,128)} %get-tuple-element.6.src_ref), channel_id=1, source_target_pairs={{0,5},{1,4},{2,7},{3,6},{4,1},{5,0},{6,3},{7,2},{8,13},{9,12},{10,... | collective-permute-start | bytes 98312 | tf_op jit(solution)/shard_map/ppermute | solution.py:303
  4.5 2.9 %collective-permute-start.1 = (f32[8,1024]{1,0:T(8,128)}, f32[8,1024]{1,0:T(8,128)S(1)}, u32[]{:S(2)}, u32[]{:S(2)}) collective-permute-start(f32[8,1024]{1,0:T(8,128)} %get-tuple-element.6.src_ref), channel_id=1, source_target_pairs={{0,9},{1,8},{2,11},{3,10},{4,13},{5,12},{6,15},{7,14},{8,1},{9,0},... | collective-permute-start | bytes 98312 | tf_op jit(solution)/shard_map/ppermute | solution.py:303
  7.4 0.0 collective-permute-start.2
  7.4 3.1 %near.1 = (f32[256,64]{1,0:T(8,128)}, f32[256,128]{1,0:T(8,128)}) custom-call(f32[8,1024]{1,0:T(8,128)} %get-tuple-element.6.src_ref, f32[16,256]{1,0:T(8,128)} %get-tuple-element.7.own_ref.refs_3_), custom_call_target="tpu_custom_call" | custom-call | flops 10485760 | bytes 400000 | tf_op jit(solution)/shard_map/near/pallas_call | solution.py:320
  10.5 0.0 collective-permute-done.refs_0_
  10.5 0.0 copy-start.2
  10.5 0.0 collective-permute-done.1.refs_1_
  10.5 0.0 copy-start.3
  10.5 2.6 %collective-permute-done.2.refs_2_ = f32[8,1024]{1,0:T(8,128)S(1)} collective-permute-done((f32[8,1024]{1,0:T(8,128)}, f32[8,1024]{1,0:T(8,128)S(1)}, u32[]{:S(2)}, u32[]{:S(2)}) %collective-permute-start.2) | collective-permute-done | bytes 32800 | tf_op jit(solution)/shard_map/ppermute | solution.py:303
  13.1 0.0 copy-start.4
  13.1 0.0 copy-done.2
  13.1 0.0 copy-done.3
  13.1 0.6 %copy-done.4 = f32[8,1024]{1,0:T(8,128)} copy-done((f32[8,1024]{1,0:T(8,128)}, f32[8,1024]{1,0:T(8,128)S(1)}, u32[]{:S(2)}) %copy-start.4) | copy-done | bytes 32792
  13.7 0.0 copy-start.5
  13.7 0.0 copy-start.6
  13.7 5.6 %far.1 = f32[16,256]{1,0:T(8,128)} custom-call(f32[8,1024]{1,0:T(8,128)} %copy-done.2, f32[8,1024]{1,0:T(8,128)} %copy-done.3, f32[8,1024]{1,0:T(8,128)} %copy-done.4, f32[16,256]{1,0:T(8,128)} %get-tuple-element.7.own_ref.refs_3_, f32[256,64]{1,0:T(8,128)} %get-tuple-element.8.refs_4_, f32[256,128]{1,0:T(8,128)} %get-tuple-element.9.refs_5_), custom_call_target="tpu_custom_call" | custom-call | tf_op jit(solution)/shard_map/far/pallas_call | solution.py:329
  19.3 0.0 copy-start
  19.3 0.0 collective-permute-start.3
  19.3 0.0 copy-done.5
  19.3 0.6 %broadcast_in_dim.14.refs_1_ = s32[1,1536]{1,0:T(1,128)} reshape(s32[1536]{0:T(1024)S(1)} %copy-done.5) | data formatting | bytes 12288 | tf_op jit(solution)/shard_map/broadcast_in_dim | solution.py:353
  19.9 0.0 copy-done.6
  19.9 0.6 %broadcast_in_dim.15.refs_2_ = s32[1,1536]{1,0:T(1,128)} reshape(s32[1536]{0:T(1024)S(1)} %copy-done.6) | data formatting | bytes 12288 | tf_op jit(solution)/shard_map/broadcast_in_dim | solution.py:353
  20.5 2.2 %collective-permute-done.3 = f32[16,256]{1,0:T(8,128)S(1)} collective-permute-done((f32[16,256]{1,0:T(8,128)}, f32[16,256]{1,0:T(8,128)S(1)}, u32[]{:S(2)}, u32[]{:S(2)}) %collective-permute-start.3) | collective-permute-done | bytes 16416 | tf_op jit(solution)/shard_map/ppermute | solution.py:303
  22.7 0.0 copy-done
  22.7 0.0 collective-permute-start.4
  22.7 4.7 %collective-permute-done.4 = f32[16,512]{1,0:T(8,128)S(1)} collective-permute-done((f32[16,512]{1,0:T(8,128)S(1)}, f32[16,512]{1,0:T(8,128)S(1)}, u32[]{:S(2)}, u32[]{:S(2)}) %collective-permute-start.4) | collective-permute-done | bytes 32800 | tf_op jit(solution)/shard_map/ppermute | solution.py:303
  27.4 1.2 %collective-permute-start.5 = (f32[16,1024]{1,0:T(8,128)S(1)}, f32[16,1024]{1,0:T(8,128)S(1)}, u32[]{:S(2)}, u32[]{:S(2)}) collective-permute-start(f32[16,1024]{1,0:T(8,128)S(1)} %pad_maximum_fusion.1), channel_id=1, source_target_pairs={{0,3},{1,2},{2,1},{3,0},{4,7},{5,6},{6,5},{7,4},{8,11},{9,10},{10,... | collective-permute-start | bytes 196616 | tf_op jit(solution)/shard_map/ppermute | solution.py:303
  28.7 2.9 %collective-permute-done.5 = f32[16,1024]{1,0:T(8,128)S(1)} collective-permute-done((f32[16,1024]{1,0:T(8,128)S(1)}, f32[16,1024]{1,0:T(8,128)S(1)}, u32[]{:S(2)}, u32[]{:S(2)}) %collective-permute-start.5) | collective-permute-done | bytes 65568 | tf_op jit(solution)/shard_map/ppermute | solution.py:303
  31.5 0.2 collective-permute-start.6
  31.7 1.2 %collective-permute-done.6 = f32[16,2048]{1,0:T(8,128)S(1)} collective-permute-done((f32[16,2048]{1,0:T(8,128)S(1)}, f32[16,2048]{1,0:T(8,128)S(1)}, u32[]{:S(2)}, u32[]{:S(2)}) %collective-permute-start.6) | collective-permute-done | bytes 131104 | tf_op jit(solution)/shard_map/ppermute | solution.py:303
  33.0 0.0 copy-start.1
  33.0 0.7 %copy-done.1 = f32[16,4096]{1,0:T(8,128)} copy-done((f32[16,4096]{1,0:T(8,128)}, f32[16,4096]{1,0:T(8,128)S(1)}, u32[]{:S(2)}) %copy-start.1) | copy-done | bytes 262168
  33.7 2.5 %pick.1 = (f32[6,1536]{1,0:T(8,128)}, f32[7,1536]{1,0:T(8,128)}) custom-call(f32[16,4096]{1,0:T(8,128)} %copy-done.1, s32[1,1536]{1,0:T(1,128)} %broadcast_in_dim.14.refs_1_, s32[1,1536]{1,0:T(1,128)} %broadcast_in_dim.15.refs_2_), custom_call_target="tpu_custom_call" | custom-call | tf_op jit(solution)/shard_map/pick/pallas_call | solution.py:347
  (8 shorter events, 0.0 us)
Async XLA Ops:
  2.1 8.4 %collective-permute-start = (f32[8,1024]{1,0:T(8,128)}, f32[8,1024]{1,0:T(8,128)S(1)}, u32[]{:S(2)}, u32[]{:S(2)}) collective-permute-start(f32[8,1024]{1,0:T(8,128)} %get-tuple-element.6.src_ref), channel_id=1, source_target_pairs={{0,5},{1,4},{2,7},{3,6},{4,1},{5,0},{6,3},{7,2},{8,13},{9,12},{10,... | collective-permute-start | bytes 98312 | tf_op jit(solution)/shard_map/ppermute | solution.py:303
  4.5 5.9 %collective-permute-start.1 = (f32[8,1024]{1,0:T(8,128)}, f32[8,1024]{1,0:T(8,128)S(1)}, u32[]{:S(2)}, u32[]{:S(2)}) collective-permute-start(f32[8,1024]{1,0:T(8,128)} %get-tuple-element.6.src_ref), channel_id=1, source_target_pairs={{0,9},{1,8},{2,11},{3,10},{4,13},{5,12},{6,15},{7,14},{8,1},{9,0},... | collective-permute-start | bytes 98312 | tf_op jit(solution)/shard_map/ppermute | solution.py:303
  7.4 5.7 %collective-permute-start.2 = (f32[8,1024]{1,0:T(8,128)}, f32[8,1024]{1,0:T(8,128)S(1)}, u32[]{:S(2)}, u32[]{:S(2)}) collective-permute-start(f32[8,1024]{1,0:T(8,128)} %get-tuple-element.6.src_ref), channel_id=1, source_target_pairs={{0,13},{1,12},{2,15},{3,14},{4,9},{5,8},{6,11},{7,10},{8,5},{9,4},... | collective-permute-start | bytes 98312 | tf_op jit(solution)/shard_map/ppermute | solution.py:303
  10.5 2.6 %copy-start.2 = (f32[8,1024]{1,0:T(8,128)}, f32[8,1024]{1,0:T(8,128)S(1)}, u32[]{:S(2)}) copy-start(f32[8,1024]{1,0:T(8,128)S(1)} %collective-permute-done.refs_0_) | copy-start | bytes 98308
  10.5 2.6 %copy-start.3 = (f32[8,1024]{1,0:T(8,128)}, f32[8,1024]{1,0:T(8,128)S(1)}, u32[]{:S(2)}) copy-start(f32[8,1024]{1,0:T(8,128)S(1)} %collective-permute-done.1.refs_1_) | copy-start | bytes 98308
  13.1 0.6 %copy-start.4 = (f32[8,1024]{1,0:T(8,128)}, f32[8,1024]{1,0:T(8,128)S(1)}, u32[]{:S(2)}) copy-start(f32[8,1024]{1,0:T(8,128)S(1)} %collective-permute-done.2.refs_2_) | copy-start | bytes 98308
  13.7 5.6 %copy-start.5 = (s32[1536]{0:T(1024)S(1)}, s32[1536]{0:T(1024)}, u32[]{:S(2)}) copy-start(s32[1536]{0:T(1024)} %param.10) | copy-start | bytes 18436
  13.7 6.2 %copy-start.6 = (s32[1536]{0:T(1024)S(1)}, s32[1536]{0:T(1024)}, u32[]{:S(2)}) copy-start(s32[1536]{0:T(1024)} %param.11) | copy-start | bytes 18436
  19.3 3.4 %copy-start = (f32[16,256]{1,0:T(8,128)S(1)}, f32[16,256]{1,0:T(8,128)}, u32[]{:S(2)}) copy-start(f32[16,256]{1,0:T(8,128)} %far.1) | copy-start | bytes 49156
  19.3 3.4 %collective-permute-start.3 = (f32[16,256]{1,0:T(8,128)}, f32[16,256]{1,0:T(8,128)S(1)}, u32[]{:S(2)}, u32[]{:S(2)}) collective-permute-start(f32[16,256]{1,0:T(8,128)} %far.1), channel_id=1, source_target_pairs={{0,5},{1,4},{2,7},{3,6},{4,1},{5,0},{6,3},{7,2},{8,13},{9,12},{10,... | collective-permute-start | bytes 49160 | tf_op jit(solution)/shard_map/ppermute | solution.py:303
  22.7 4.8 %collective-permute-start.4 = (f32[16,512]{1,0:T(8,128)S(1)}, f32[16,512]{1,0:T(8,128)S(1)}, u32[]{:S(2)}, u32[]{:S(2)}) collective-permute-start(f32[16,512]{1,0:T(8,128)S(1)} %pad_maximum_fusion.2), channel_id=1, source_target_pairs={{0,9},{1,8},{2,11},{3,10},{4,13},{5,12},{6,15},{7,14},{8,1},{9,0},... | collective-permute-start | bytes 98312 | tf_op jit(solution)/shard_map/ppermute | solution.py:303
  27.4 4.1 %collective-permute-start.5 = (f32[16,1024]{1,0:T(8,128)S(1)}, f32[16,1024]{1,0:T(8,128)S(1)}, u32[]{:S(2)}, u32[]{:S(2)}) collective-permute-start(f32[16,1024]{1,0:T(8,128)S(1)} %pad_maximum_fusion.1), channel_id=1, source_target_pairs={{0,3},{1,2},{2,1},{3,0},{4,7},{5,6},{6,5},{7,4},{8,11},{9,10},{10,... | collective-permute-start | bytes 196616 | tf_op jit(solution)/shard_map/ppermute | solution.py:303
  31.5 1.4 %collective-permute-start.6 = (f32[16,2048]{1,0:T(8,128)S(1)}, f32[16,2048]{1,0:T(8,128)S(1)}, u32[]{:S(2)}, u32[]{:S(2)}) collective-permute-start(f32[16,2048]{1,0:T(8,128)S(1)} %pad_maximum_fusion), channel_id=1, source_target_pairs={{0,1},{1,0},{2,3},{3,2},{4,5},{5,4},{6,7},{7,6},{8,9},{9,8},{10,11... | collective-permute-start | bytes 393224 | tf_op jit(solution)/shard_map/ppermute | solution.py:303
  33.0 0.7 %copy-start.1 = (f32[16,4096]{1,0:T(8,128)}, f32[16,4096]{1,0:T(8,128)S(1)}, u32[]{:S(2)}) copy-start(f32[16,4096]{1,0:T(8,128)S(1)} %constant_dynamic-update-slice_fusion.refs_0_) | copy-start | bytes 786436

commit v2 on v1

--- a/solution.py
+++ b/solution.py
@@ -12,6 +12,7 @@
 ROWS = 16
 COLS = 64
 VMEM = pl.BlockSpec(memory_space=pltpu.VMEM)
+PARAMS = pltpu.CompilerParams(vmem_limit_bytes=16 << 20)
 BOTH_MINOR = (((1,), (1,)), ((), ()))
 
 
@@ -95,7 +96,17 @@
     return (jnp.concatenate([position, velocity], axis=0), forces)
 
 
-def predict_kernel(pv_ref, aj_ref, mass_ref, age_ref, src_ref, own_ref):
+def predict_kernel(pv_hbm, aj_hbm, mass_hbm, age_hbm, src_ref, own_ref, pv_ref, aj_ref, mass_ref, age_ref, sems):
+    copies = [
+        pltpu.make_async_copy(hbm, ref, sems.at[i])
+        for i, (hbm, ref) in enumerate(
+            ((pv_hbm, pv_ref), (aj_hbm, aj_ref), (mass_hbm, mass_ref), (age_hbm, age_ref))
+        )
+    ]
+    for copy in copies:
+        copy.start()
+    for copy in copies:
+        copy.wait()
     width = own_ref.shape[1]
     step_len = age_ref[...]
     accel = aj_ref[0:3, :]
@@ -255,36 +266,36 @@
     out_ref[15:16, :] = jnp.zeros((1, width), f32)
 
 
-def pick_kernel(ia_bits, ja_bits, width, table_ref, local_ref, owner_ref, state_ref, forces_ref):
-    count = local_ref.shape[1]
+def pick_kernel(ia_bits, ja_bits, width, first_slot, last, refs):
+    table_ref, local_ref, owner_ref = refs[:3]
+    before = refs[3:-2]
+    state_ref, forces_ref = refs[-2:]
+    count = local_ref.shape[0]
     per = width // LANES
     my_ja = lax.axis_index("ja")
     my_ia = lax.axis_index("ia")
     for b in range(count // LANES):
         cs = slice(b * LANES, b * LANES + LANES)
-        local = local_ref[:, cs]
-        apart_ja = lax.bitwise_xor(owner_ref[:, cs], my_ja)
+        local = local_ref[cs].reshape(1, LANES)
+        apart_ja = lax.bitwise_xor(owner_ref[cs].reshape(1, LANES), my_ja)
         apart_ia = lax.bitwise_xor(local // width, my_ia)
-        parity = apart_ia
+        flips = apart_ia + (apart_ja != 0).astype(jnp.int32)
         for i in range(1, ia_bits):
-            parity = lax.bitwise_xor(parity, lax.shift_right_logical(apart_ia, i))
-        flips = parity
-        for i in range(ja_bits):
-            flips = lax.bitwise_xor(flips, lax.shift_right_logical(apart_ja, i))
+            flips = flips + lax.shift_right_logical(apart_ia, i)
         slot = apart_ja + lax.shift_left(lax.shift_right_logical(apart_ia, 1), ja_bits)
         slot = slot + lax.shift_left(lax.bitwise_and(flips, 1), ja_bits + ia_bits - 1)
         within = lax.rem(local, width)
-        piece = jnp.broadcast_to(slot * per + within // LANES, (8, LANES))
+        piece = jnp.broadcast_to((slot - first_slot) * per + within // LANES, (8, LANES))
         lane = jnp.broadcast_to(lax.rem(within, LANES), (8, LANES))
-        state = jnp.zeros((8, LANES), f32)
-        forces = jnp.zeros((8, LANES), f32)
+        state = before[0][:, cs] if before else jnp.zeros((8, LANES), f32)
+        forces = before[1][:, cs] if before else jnp.zeros((8, LANES), f32)
         for t in range(table_ref.shape[1] // LANES):
             hit = piece == t
             ts = slice(t * LANES, t * LANES + LANES)
             state = jnp.where(hit, jnp.take_along_axis(table_ref[0:8, ts], lane, axis=1), state)
             forces = jnp.where(hit, jnp.take_along_axis(table_ref[8:16, ts], lane, axis=1), forces)
-        state_ref[:, cs] = state[0:6, :]
-        forces_ref[:, cs] = forces[0:7, :]
+        state_ref[:, cs] = state[0 : state_ref.shape[0], :]
+        forces_ref[:, cs] = forces[0 : forces_ref.shape[0], :]
 
 
 def shape_of(*dims):
@@ -305,10 +316,18 @@
     src, own = pl.pallas_call(
         predict_kernel,
         out_shape=(shape_of(8, stars), shape_of(16, width)),
-        in_specs=[VMEM] * 4,
+        in_specs=[pl.BlockSpec(memory_space=pltpu.HBM)] * 4,
         out_specs=(VMEM, VMEM),
+        scratch_shapes=[
+            pltpu.VMEM((6, stars), f32),
+            pltpu.VMEM((6, stars), f32),
+            pltpu.VMEM((1, stars), f32),
+            pltpu.VMEM((1, stars), f32),
+            pltpu.SemaphoreType.DMA((4,)),
+        ],
+        compiler_params=PARAMS,
         name="predict",
-    )(pos_vel, acc_jerk, mass[None, :], age[None, :])
+    )(*(pltpu.with_memory_space_constraint(x, pltpu.HBM) for x in (pos_vel, acc_jerk, mass[None, :], age[None, :])))
     others = [exchange(src, d, 1) for d in range(1, nj)]
     scratch = [
         pltpu.VMEM((2, COLS, stars), f32),
@@ -324,6 +343,7 @@
         out_specs=(VMEM, VMEM),
         scratch_shapes=scratch,
         cost_estimate=pairs_cost,
+        compiler_params=PARAMS,
         name="near",
     )(src, own)
     block = pl.pallas_call(
@@ -332,25 +352,33 @@
         in_specs=[VMEM] * (len(others) + 3),
         out_specs=VMEM,
         scratch_shapes=scratch,
+        compiler_params=PARAMS,
         name="far",
     )(*others, own, sums, pot)
-    for bit in range(ja_bits):
-        block = jnp.concatenate([block, exchange(block, 1 << bit, 1)], axis=1)
-    for bit in range(1, ia_bits):
-        block = jnp.concatenate([block, exchange(block, 0, (1 << bit) + 1)], axis=1)
-    block = jnp.concatenate([block, exchange(block, 0, 1)], axis=1)
     count = active_local.shape[0]
 
-    def pick(*refs):
-        pick_kernel(ia_bits, ja_bits, width, *refs)
-
-    return pl.pallas_call(
-        pick,
-        out_shape=(shape_of(6, count), shape_of(7, count)),
-        in_specs=[VMEM] * 3,
-        out_specs=(VMEM, VMEM),
-        name="pick",
-    )(block, active_local[None, :], active_owner[None, :])
+    def pick(table, first_slot, before, last=False):
+        return pl.pallas_call(
+            lambda *refs: pick_kernel(ia_bits, ja_bits, width, first_slot, last, refs),
+            out_shape=(shape_of(6 if last else 8, count), shape_of(7 if last else 8, count)),
+            in_specs=[VMEM] * (3 + len(before)),
+            out_specs=(VMEM, VMEM),
+            compiler_params=PARAMS,
+            cost_estimate=pl.CostEstimate(flops=count * table.shape[1], transcendentals=0, bytes_accessed=400000),
+            name="pick",
+        )(table, active_local, active_owner, *before)
+
+    table = jnp.concatenate([block, *(exchange(block, d, 1) for d in range(1, nj))], axis=1)
+    slots = nj
+    fresh, first_slot, found = table, 0, ()
+    for step in [(1 << bit) + 1 for bit in range(1, ia_bits)] + [1]:
+        came = exchange(table, 0, step)
+        found = pick(fresh, first_slot, found)
+        fresh, first_slot = came, slots
+        if step != 1:
+            table = jnp.concatenate([table, came], axis=1)
+        slots *= 2
+    return tuple(pick(fresh, first_slot, found, True))
 
 
 def solution(mesh):
@@ -363,7 +391,7 @@
         fits = (
             nj & (nj - 1) == 0
             and ni & (ni - 1) == 0
-            and nj > 1
+            and 1 < nj <= 8
             and ni > 1
             and stars % ni == 0
             and width % LANES == 0

time: 36.5 us -> 28.3 us (0.78)
  waiting for transfers between devices: 13.6 us -> 7.88 us
  starting transfers between devices: 6.76 us -> 11.4 us
  Pallas kernels: 12.6 us -> 8.1 us
  local copies, waits for them, and re-layouts: 2.54 us -> 0.02 us
    ppermute x7 -> x8, waiting for transfers between devices: 13.6 us -> 7.88 us  [exchange(): return lax.ppermute(x, ('ja', 'ia'), pairs)]
    ppermute x7 -> x8, starting transfers between devices: 6.76 us -> 11.4 us  [exchange(): return lax.ppermute(x, ('ja', 'ia'), pairs)]
    pallas_call x1, Pallas kernels: 5.57 us -> 3.9 us  [all_stars(): pl.pallas_call(remote_kernel, out_shape=shape_of(16, width), in_specs=[VM...]
    pallas_call x1, Pallas kernels: 3.06 us -> 1.57 us  [all_stars(): pl.pallas_call(local_kernel, out_shape=(shape_of(width, COLS), shape_of(w...]
    unnamed x18 -> x8, local copies, waits for them, and re-layouts: 1.33 us -> 0.02 us
    broadcast_in_dim x2 -> x0, local copies, waits for them, and re-layouts: 1.2 us -> none  [the longest x1 0.6 us: all_stars(): active_local[None, :]]
    pallas_call x1 -> x3, Pallas kernels: 2.51 us -> 1.78 us  [pick(): pl.pallas_call(lambda *refs: pick_kernel(ia_bits, ja_bits, width, first_s...]
    pallas_call x1, Pallas kernels: 1.42 us -> 0.84 us  [all_stars(): pl.pallas_call(predict_kernel, out_shape=(shape_of(8, stars), shape_of(16...]
  transfers between devices with their start and end apart: 7 -> 8, of which waited for: 5 -> 5; matrix products, arithmetic and copies ran while one was open for 3% -> 0% of each run, Pallas kernels for 8% -> 8%
where the time goes in v2:
time: 28.3 us; the launch traced here: 28.1 us
  starting transfers between devices  11.4 us (40%)
  Pallas kernels  8.1 us (29%)
  waiting for transfers between devices  7.88 us (28%)
  between operations  0.69 us (2%)
    ppermute x8, starting transfers between devices, exchange(): return lax.ppermute(x, ('ja', 'ia'), pairs)  11.4 us
    ppermute x8, waiting for transfers between devices, exchange(): return lax.ppermute(x, ('ja', 'ia'), pairs)  7.88 us
    pallas_call x1, Pallas kernels, all_stars(): pl.pallas_call(remote_kernel, out_shape=shape_of(16, width), in_specs=[VM...  3.9 us
    pallas_call x3, Pallas kernels, pick(): pl.pallas_call(lambda *refs: pick_kernel(ia_bits, ja_bits, width, first_s...  1.78 us
    pallas_call x1, Pallas kernels, all_stars(): pl.pallas_call(local_kernel, out_shape=(shape_of(width, COLS), shape_of(w...  1.57 us
    pallas_call x1, Pallas kernels, all_stars(): pl.pallas_call(predict_kernel, out_shape=(shape_of(8, stars), shape_of(16...  0.84 us
  transfers between devices with their start and end apart: 8, of which 5 were waited for; matrix products, arithmetic and copies ran while one was open for 0% of the time, Pallas kernels for 8%

profile of v2, /device:TPU:0, one launch (start us, length us, event | category | flops | bytes accessed | tf_op | source)
XLA Modules:
  0.0 28.1 jit_solution(8127957816834435044)
XLA Ops:
  0.6 0.8 %predict.1 = (f32[8,1024]{1,0:T(8,128)S(1)}, f32[16,256]{1,0:T(8,128)S(1)}) custom-call(f32[6,1024]{1,0:T(8,128)} %pv_hbm.1, f32[6,1024]{1,0:T(8,128)} %aj_hbm.1, f32[1,1024]{1,0:T(1,128)} %bitcast.2, f32[1,1024]{1,0:T(1,128)} %bitcast.3), custom_call_target="tpu_custom_call" | custom-call | tf_op jit(solution)/shard_map/predict/pallas_call | solution.py:316
  1.5 2.6 %collective-permute-start = (f32[8,1024]{1,0:T(8,128)S(1)}, f32[8,1024]{1,0:T(8,128)S(1)}, u32[]{:S(2)}, u32[]{:S(2)}) collective-permute-start(f32[8,1024]{1,0:T(8,128)S(1)} %get-tuple-element.10.src_ref), channel_id=1, source_target_pairs={{0,5},{1,4},{2,7},{3,6},{4,1},{5,0},{6,3},{7,2},{8,13},{9,12},{10,... | collective-permute-start | bytes 98312 | tf_op jit(solution)/shard_map/ppermute | solution.py:314
  4.0 2.9 %collective-permute-start.1 = (f32[8,1024]{1,0:T(8,128)S(1)}, f32[8,1024]{1,0:T(8,128)S(1)}, u32[]{:S(2)}, u32[]{:S(2)}) collective-permute-start(f32[8,1024]{1,0:T(8,128)S(1)} %get-tuple-element.10.src_ref), channel_id=1, source_target_pairs={{0,9},{1,8},{2,11},{3,10},{4,13},{5,12},{6,15},{7,14},{8,1},{9,0},... | collective-permute-start | bytes 98312 | tf_op jit(solution)/shard_map/ppermute | solution.py:314
  6.9 0.0 collective-permute-start.2
  6.9 1.6 %near.1 = (f32[256,64]{1,0:T(8,128)S(1)}, f32[256,128]{1,0:T(8,128)S(1)}) custom-call(f32[8,1024]{1,0:T(8,128)S(1)} %get-tuple-element.10.src_ref, f32[16,256]{1,0:T(8,128)S(1)} %get-tuple-element.11.own_ref.refs_3_), custom_call_target="tpu_custom_call" | custom-call | flops 10485760 | bytes 400000 | tf_op jit(solution)/shard_map/near/pallas_call | solution.py:339
  8.5 0.0 collective-permute-done.refs_0_
  8.5 0.0 collective-permute-done.1.refs_1_
  8.5 3.9 %collective-permute-done.2.refs_2_ = f32[8,1024]{1,0:T(8,128)S(1)} collective-permute-done((f32[8,1024]{1,0:T(8,128)S(1)}, f32[8,1024]{1,0:T(8,128)S(1)}, u32[]{:S(2)}, u32[]{:S(2)}) %collective-permute-start.2) | collective-permute-done | bytes 32800 | tf_op jit(solution)/shard_map/ppermute | solution.py:314
  12.4 3.9 %far.1 = f32[16,256]{1,0:T(8,128)S(1)} custom-call(f32[8,1024]{1,0:T(8,128)S(1)} %collective-permute-done.refs_0_, f32[8,1024]{1,0:T(8,128)S(1)} %collective-permute-done.1.refs_1_, f32[8,1024]{1,0:T(8,128)S(1)} %collective-permute-done.2.refs_2_, f32[16,256]{1,0:T(8,128)S(1)} %get-tuple-element.11.own_ref.refs_3_, f32[256,64]{1,0:T(8,128)S(1)} %get-tuple-element.12.refs_4_, ...), custom_call_target="tpu_custom_call" | custom-call | tf_op jit(solution)/shard_map/far/pallas_call | solution.py:349
  16.3 0.1 collective-permute-start.3
  16.4 0.1 collective-permute-start.4
  16.5 3.7 %collective-permute-start.5 = (f32[16,256]{1,0:T(8,128)S(1)}, f32[16,256]{1,0:T(8,128)S(1)}, u32[]{:S(2)}, u32[]{:S(2)}) collective-permute-start(f32[16,256]{1,0:T(8,128)S(1)} %far.1), channel_id=1, source_target_pairs={{0,13},{1,12},{2,15},{3,14},{4,9},{5,8},{6,11},{7,10},{8,5},{9,4},... | collective-permute-start | bytes 49160 | tf_op jit(solution)/shard_map/ppermute | solution.py:314
  20.2 0.0 collective-permute-done.3
  20.2 0.3 %collective-permute-done.4 = f32[16,256]{1,0:T(8,128)S(1)} collective-permute-done((f32[16,256]{1,0:T(8,128)S(1)}, f32[16,256]{1,0:T(8,128)S(1)}, u32[]{:S(2)}, u32[]{:S(2)}) %collective-permute-start.4) | collective-permute-done | bytes 16416 | tf_op jit(solution)/shard_map/ppermute | solution.py:314
  20.5 1.3 %collective-permute-done.5 = f32[16,256]{1,0:T(8,128)S(1)} collective-permute-done((f32[16,256]{1,0:T(8,128)S(1)}, f32[16,256]{1,0:T(8,128)S(1)}, u32[]{:S(2)}, u32[]{:S(2)}) %collective-permute-start.5) | collective-permute-done | bytes 16416 | tf_op jit(solution)/shard_map/ppermute | solution.py:314
  21.8 1.6 %collective-permute-start.6 = (f32[16,1024]{1,0:T(8,128)S(1)}, f32[16,1024]{1,0:T(8,128)S(1)}, u32[]{:S(2)}, u32[]{:S(2)}) collective-permute-start(f32[16,1024]{1,0:T(8,128)S(1)} %pad_maximum_fusion.refs_0_), channel_id=1, source_target_pairs={{0,3},{1,2},{2,1},{3,0},{4,7},{5,6},{6,5},{7,4},{8,11},{9,10},{10,... | collective-permute-start | bytes 196616 | tf_op jit(solution)/shard_map/ppermute | solution.py:314
  23.4 0.0 copy-start
  23.4 0.0 copy-start.1
  23.4 2.1 %collective-permute-done.6.refs_0_ = f32[16,1024]{1,0:T(8,128)S(1)} collective-permute-done((f32[16,1024]{1,0:T(8,128)S(1)}, f32[16,1024]{1,0:T(8,128)S(1)}, u32[]{:S(2)}, u32[]{:S(2)}) %collective-permute-start.6) | collective-permute-done | bytes 65568 | tf_op jit(solution)/shard_map/ppermute | solution.py:314
  25.5 0.5 %collective-permute-start.7 = (f32[16,2048]{1,0:T(8,128)S(1)}, f32[16,2048]{1,0:T(8,128)S(1)}, u32[]{:S(2)}, u32[]{:S(2)}) collective-permute-start(f32[16,2048]{1,0:T(8,128)S(1)} %constant_dynamic-update-slice_fusion), channel_id=1, source_target_pairs={{0,1},{1,0},{2,3},{3,2},{4,5},{5,4},{6,7},{7,6},{8,9},{9,8},{10,11... | collective-permute-start | bytes 393224 | tf_op jit(solution)/shard_map/ppermute | solution.py:314
  26.0 0.0 copy-done
  26.0 0.0 copy-done.1
  26.0 0.3 %pick.3 = (f32[8,1536]{1,0:T(8,128)S(1)}, f32[8,1536]{1,0:T(8,128)S(1)}) custom-call(f32[16,1024]{1,0:T(8,128)S(1)} %pad_maximum_fusion.refs_0_, s32[1536]{0:T(1024)S(1)} %copy-done, s32[1536]{0:T(1024)S(1)} %copy-done.1), custom_call_target="tpu_custom_call" | custom-call | flops 1572864 | bytes 400000 | tf_op jit(solution)/shard_map/pick/pallas_call | solution.py:361
  26.3 0.3 %pick.4 = (f32[8,1536]{1,0:T(8,128)S(1)}, f32[8,1536]{1,0:T(8,128)S(1)}) custom-call(f32[16,1024]{1,0:T(8,128)S(1)} %collective-permute-done.6.refs_0_, s32[1536]{0:T(1024)S(1)} %copy-done, s32[1536]{0:T(1024)S(1)} %copy-done.1, f32[8,1536]{1,0:T(8,128)S(1)} %get-tuple-element.14.refs_3_, f32[8,1536]{1,0:T(8,128)S(1)} %get-tuple-element.15.refs_4_), custom_call_target="tpu_custom_call" | custom-call | flops 1572864 | bytes 400000 | tf_op jit(solution)/shard_map/pick/pallas_call | solution.py:361
  26.7 0.3 %collective-permute-done.7.refs_0_ = f32[16,2048]{1,0:T(8,128)S(1)} collective-permute-done((f32[16,2048]{1,0:T(8,128)S(1)}, f32[16,2048]{1,0:T(8,128)S(1)}, u32[]{:S(2)}, u32[]{:S(2)}) %collective-permute-start.7) | collective-permute-done | bytes 131104 | tf_op jit(solution)/shard_map/ppermute | solution.py:314
  27.0 1.1 %pick.5 = (f32[6,1536]{1,0:T(8,128)}, f32[7,1536]{1,0:T(8,128)}) custom-call(f32[16,2048]{1,0:T(8,128)S(1)} %collective-permute-done.7.refs_0_, s32[1536]{0:T(1024)S(1)} %copy-done, s32[1536]{0:T(1024)S(1)} %copy-done.1, f32[8,1536]{1,0:T(8,128)S(1)} %get-tuple-element.16.refs_3_, f32[8,1536]{1,0:T(8,128)S(1)} %get-tuple-element.17.refs_4_), custom_call_target="tpu_custom_call" | custom-call | flops 3145728 | bytes 400000 | tf_op jit(solution)/shard_map/pick/pallas_call | solution.py:361
  (6 shorter events, 0.0 us)
Async XLA Ops:
  1.5 7.0 %collective-permute-start = (f32[8,1024]{1,0:T(8,128)S(1)}, f32[8,1024]{1,0:T(8,128)S(1)}, u32[]{:S(2)}, u32[]{:S(2)}) collective-permute-start(f32[8,1024]{1,0:T(8,128)S(1)} %get-tuple-element.10.src_ref), channel_id=1, source_target_pairs={{0,5},{1,4},{2,7},{3,6},{4,1},{5,0},{6,3},{7,2},{8,13},{9,12},{10,... | collective-permute-start | bytes 98312 | tf_op jit(solution)/shard_map/ppermute | solution.py:314
  4.0 4.5 %collective-permute-start.1 = (f32[8,1024]{1,0:T(8,128)S(1)}, f32[8,1024]{1,0:T(8,128)S(1)}, u32[]{:S(2)}, u32[]{:S(2)}) collective-permute-start(f32[8,1024]{1,0:T(8,128)S(1)} %get-tuple-element.10.src_ref), channel_id=1, source_target_pairs={{0,9},{1,8},{2,11},{3,10},{4,13},{5,12},{6,15},{7,14},{8,1},{9,0},... | collective-permute-start | bytes 98312 | tf_op jit(solution)/shard_map/ppermute | solution.py:314
  6.9 5.5 %collective-permute-start.2 = (f32[8,1024]{1,0:T(8,128)S(1)}, f32[8,1024]{1,0:T(8,128)S(1)}, u32[]{:S(2)}, u32[]{:S(2)}) collective-permute-start(f32[8,1024]{1,0:T(8,128)S(1)} %get-tuple-element.10.src_ref), channel_id=1, source_target_pairs={{0,13},{1,12},{2,15},{3,14},{4,9},{5,8},{6,11},{7,10},{8,5},{9,4},... | collective-permute-start | bytes 98312 | tf_op jit(solution)/shard_map/ppermute | solution.py:314
  16.3 3.9 %collective-permute-start.3 = (f32[16,256]{1,0:T(8,128)S(1)}, f32[16,256]{1,0:T(8,128)S(1)}, u32[]{:S(2)}, u32[]{:S(2)}) collective-permute-start(f32[16,256]{1,0:T(8,128)S(1)} %far.1), channel_id=1, source_target_pairs={{0,5},{1,4},{2,7},{3,6},{4,1},{5,0},{6,3},{7,2},{8,13},{9,12},{10,... | collective-permute-start | bytes 49160 | tf_op jit(solution)/shard_map/ppermute | solution.py:314
  16.4 4.1 %collective-permute-start.4 = (f32[16,256]{1,0:T(8,128)S(1)}, f32[16,256]{1,0:T(8,128)S(1)}, u32[]{:S(2)}, u32[]{:S(2)}) collective-permute-start(f32[16,256]{1,0:T(8,128)S(1)} %far.1), channel_id=1, source_target_pairs={{0,9},{1,8},{2,11},{3,10},{4,13},{5,12},{6,15},{7,14},{8,1},{9,0},... | collective-permute-start | bytes 49160 | tf_op jit(solution)/shard_map/ppermute | solution.py:314
  16.5 5.3 %collective-permute-start.5 = (f32[16,256]{1,0:T(8,128)S(1)}, f32[16,256]{1,0:T(8,128)S(1)}, u32[]{:S(2)}, u32[]{:S(2)}) collective-permute-start(f32[16,256]{1,0:T(8,128)S(1)} %far.1), channel_id=1, source_target_pairs={{0,13},{1,12},{2,15},{3,14},{4,9},{5,8},{6,11},{7,10},{8,5},{9,4},... | collective-permute-start | bytes 49160 | tf_op jit(solution)/shard_map/ppermute | solution.py:314
  21.8 3.7 %collective-permute-start.6 = (f32[16,1024]{1,0:T(8,128)S(1)}, f32[16,1024]{1,0:T(8,128)S(1)}, u32[]{:S(2)}, u32[]{:S(2)}) collective-permute-start(f32[16,1024]{1,0:T(8,128)S(1)} %pad_maximum_fusion.refs_0_), channel_id=1, source_target_pairs={{0,3},{1,2},{2,1},{3,0},{4,7},{5,6},{6,5},{7,4},{8,11},{9,10},{10,... | collective-permute-start | bytes 196616 | tf_op jit(solution)/shard_map/ppermute | solution.py:314
  23.4 2.6 %copy-start = (s32[1536]{0:T(1024)S(1)}, s32[1536]{0:T(1024)}, u32[]{:S(2)}) copy-start(s32[1536]{0:T(1024)} %refs_1_.5) | copy-start | bytes 18436
  23.4 2.6 %copy-start.1 = (s32[1536]{0:T(1024)S(1)}, s32[1536]{0:T(1024)}, u32[]{:S(2)}) copy-start(s32[1536]{0:T(1024)} %refs_2_.5) | copy-start | bytes 18436
  25.5 1.5 %collective-permute-start.7 = (f32[16,2048]{1,0:T(8,128)S(1)}, f32[16,2048]{1,0:T(8,128)S(1)}, u32[]{:S(2)}, u32[]{:S(2)}) collective-permute-start(f32[16,2048]{1,0:T(8,128)S(1)} %constant_dynamic-update-slice_fusion), channel_id=1, source_target_pairs={{0,1},{1,0},{2,3},{3,2},{4,5},{5,4},{6,7},{7,6},{8,9},{9,8},{10,11... | collective-permute-start | bytes 393224 | tf_op jit(solution)/shard_map/ppermute | solution.py:314

commit v3 on v2

--- a/solution.py
+++ b/solution.py
@@ -96,7 +96,7 @@
     return (jnp.concatenate([position, velocity], axis=0), forces)
 
 
-def predict_kernel(pv_hbm, aj_hbm, mass_hbm, age_hbm, src_ref, own_ref, pv_ref, aj_ref, mass_ref, age_ref, sems):
+def predict_kernel(pv_hbm, aj_hbm, mass_hbm, age_hbm, src_ref, long_ref, own_ref, mid_ref, pv_ref, aj_ref, mass_ref, age_ref, sems):
     copies = [
         pltpu.make_async_copy(hbm, ref, sems.at[i])
         for i, (hbm, ref) in enumerate(
@@ -108,6 +108,7 @@
     for copy in copies:
         copy.wait()
     width = own_ref.shape[1]
+    stars = src_ref.shape[1]
     step_len = age_ref[...]
     accel = aj_ref[0:3, :]
     jolt = aj_ref[3:6, :]
@@ -116,11 +117,17 @@
     src_ref[3:6, :] = velocity + step_len * (accel + step_len * jolt * 0.5)
     src_ref[6:7, :] = mass_ref[...]
     src_ref[7:8, :] = step_len
-    mine = pl.ds(pl.multiple_of(lax.axis_index("ia") * width, LANES), width)
-    own_ref[0:6, :] = src_ref[0:6, mine]
-    own_ref[6:12, :] = aj_ref[:, mine]
-    own_ref[12:13, :] = age_ref[:, mine]
-    own_ref[13:16, :] = jnp.zeros((3, width), f32)
+    long_ref[:, 0:stars] = src_ref[...]
+    rank = lax.axis_index("ia")
+    mine = pl.ds(pl.multiple_of(rank * width, LANES), width)
+    partner = pl.ds(pl.multiple_of(lax.bitwise_xor(rank, 1) * width, LANES), width)
+    long_ref[0:6, stars : stars + width] = aj_ref[:, partner]
+    long_ref[6:8, stars : stars + width] = jnp.zeros((2, width), f32)
+    own_ref[0:8, :] = src_ref[:, mine]
+    own_ref[8:14, :] = aj_ref[:, mine]
+    own_ref[14:16, :] = jnp.zeros((2, width), f32)
+    mean = jnp.sum(src_ref[:, mine], axis=1, keepdims=True) * (1.0 / width)
+    mid_ref[...] = jnp.broadcast_to(mean, (8, LANES))
 
 
 def three_parts(x):
@@ -130,54 +137,82 @@
     return high, mid, rest - mid
 
 
-def spread_targets(own_ref, wide):
+def centred(rows, mid_ref):
+    middle = jnp.concatenate([mid_ref[...]] * (rows.shape[1] // LANES), axis=1)
+    return rows[0:3, :] - middle[0:3, :], rows[3:6, :] - middle[3:6, :]
+
+
+def dot_parts(a, b):
+    return three_parts(jnp.sum(a * b, axis=0, keepdims=True))
+
+
+def set_targets(own_ref, mid_ref, wide, near_feat, rows_ref):
     width = own_ref.shape[1]
     turned = jnp.transpose(own_ref[0:8, :])
-    for c in range(6):
+    for c in range(3):
         wide[c] = jnp.broadcast_to(turned[:, c : c + 1], (width, LANES))
-
-
-def clear_features(feat):
+    pos, vel = centred(own_ref[0:6, :], mid_ref)
+    rows_ref[...] = jnp.zeros(rows_ref.shape, f32)
+    row = 0
+    for high, mid, low in (three_parts(-vel), three_parts(-pos)):
+        for x in (high, high, mid, high, mid, low):
+            rows_ref[row : row + 3, :] = x
+            row += 3
+    rows_ref[row : row + 3, :] = jnp.ones((3, width), f32)
+    for i, x in enumerate(dot_parts(pos, vel)):
+        rows_ref[row + 3 + i : row + 4 + i, :] = x
+    near_feat[...] = jnp.transpose(rows_ref[...])
+
+
+def set_sources(src_ref, mid_ref, feat, right, far_feat, width):
     count = feat.shape[2]
+    pos, vel = centred(src_ref[0:6, 0:count], mid_ref)
+    pos_parts = three_parts(pos)
+    vel_parts = three_parts(vel)
+    one = jnp.ones((3, count), f32)
     feat[...] = jnp.zeros(feat.shape, f32)
-    one = jnp.ones((1, count), f32)
-    feat[0, 18:19, :] = one
-    feat[1, 41:42, :] = one
-
-
-def source_features(source, feat, right, width):
-    rows = 0
-    for x in (*three_parts(source[0:3, :]), *three_parts(source[3:6, :])):
-        feat[0, rows : rows + 3, :] = x
-        if rows < 9:
-            feat[1, 32 + rows : 35 + rows, :] = x
-        rows += 3
+    for i, x in enumerate((*pos_parts, *vel_parts)):
+        feat[0, 3 * i : 3 * i + 3, :] = x
+    feat[0, 18:19, :] = one[0:1, :]
+    for i, x in enumerate(pos_parts):
+        feat[1, 32 + 3 * i : 35 + 3 * i, :] = x
+    feat[1, 41:42, :] = one[0:1, :]
+    row = 0
+    for high, mid, low in (pos_parts, vel_parts):
+        for x in (high, mid, high, low, mid, high):
+            feat[2, row : row + 3, :] = x
+            row += 3
+    for i, x in enumerate(dot_parts(pos, vel)):
+        feat[2, row + i : row + i + 1, :] = x
+    feat[2, row + 3 : row + 6, :] = one
     for k in range(right.shape[0]):
+        cs = slice(k * width, k * width + width)
         for i in range(4):
-            right[k, :, i * width : i * width + width] = feat[i // 2, :, k * width : k * width + width].astype(bf16)
-
-
-def pair_chunk(source, offset, wide, left, pot_ref, diagonal):
+            right[k, :, i * width : i * width + width] = feat[i // 2, :, cs].astype(bf16)
+        far_feat[k] = feat[2, :, cs].astype(bf16)
+
+
+def pair_chunk(source, offset, flow, wide, left, pot_ref, shift):
     width = wide.shape[1]
     for rb in range(width // ROWS):
         rs = slice(rb * ROWS, rb * ROWS + ROWS)
-        target = [wide[c, rs, :] for c in range(6)]
+        target = [wide[c, rs, :] for c in range(3)]
         pot = pot_ref[rs, :]
         for j in range(width // LANES):
-            cs = pl.ds(offset + LANES * j, LANES)
-            row = [jnp.broadcast_to(source[c : c + 1, cs], (ROWS, LANES)) for c in range(7)]
-            dx, dy, dz = (row[c] - target[c] for c in range(3))
-            ex, ey, ez = (row[c] - target[c] for c in range(3, 6))
+            cs = slice(offset + LANES * j, offset + LANES * j + LANES)
+            dx, dy, dz = (
+                jnp.broadcast_to(source[c : c + 1, cs], (ROWS, LANES)) - target[c] for c in range(3)
+            )
             inverse = lax.rsqrt(((dx * dx + soften) + dy * dy) + dz * dz)
             inv_sq = inverse * inverse
-            weighted = row[6] * inverse
+            weighted = jnp.broadcast_to(source[6:7, cs], (ROWS, LANES)) * inverse
             pot = pot + weighted
             cube = weighted * inv_sq
-            if diagonal and rb * ROWS // LANES == j:
-                here = lax.broadcasted_iota(jnp.int32, (ROWS, LANES), 0) + (rb * ROWS - j * LANES)
+            if shift is not None and rb * ROWS // LANES == j:
+                here = lax.broadcasted_iota(jnp.int32, (ROWS, LANES), 0) + (rb * ROWS - j * LANES + shift)
                 there = lax.broadcasted_iota(jnp.int32, (ROWS, LANES), 1)
                 cube = jnp.where(here == there, 0.0, cube)
-            radial = cube * ((dx * ex + dy * ey + dz * ez) * inv_sq)
+            radial = cube * (flow[rs, LANES * j : LANES * j + LANES] * inv_sq)
             parts = (
                 cube,
                 cube - cube.astype(bf16).astype(f32),
@@ -193,77 +228,98 @@
     sum_ref[...] += lax.dot_general(left[...].astype(bf16), right, BOTH_MINOR, preferred_element_type=f32)
 
 
-def local_kernel(src_ref, own_ref, sum_ref, pot_ref, feat, right, wide, left):
-    width = own_ref.shape[1]
+def pair_block(source, wide, near_feat, sum_ref, pot_ref, right, far_feat, left, flow, own_block):
+    width = wide.shape[1]
     chunks = right.shape[0]
-    spread_targets(own_ref, wide)
-    clear_features(feat)
-    source_features(src_ref, feat, right, width)
+    rank = lax.axis_index("ia")
+    mine = near_feat[...].astype(bf16)
+
+    def set_flow(k):
+        flow[k % 2] = jnp.dot(mine, far_feat[k], preferred_element_type=f32)
+
+    set_flow(0)
+    for k in range(chunks):
+        if k + 1 < chunks:
+            set_flow(k + 1)
+        if k:
+            add_chunk(left.at[(k - 1) % 2], right[k - 1], sum_ref)
+        shift = jnp.where(rank == k, 0, width) if own_block else None
+        pair_chunk(source, k * width, flow.at[k % 2], wide, left.at[k % 2], pot_ref, shift)
+    add_chunk(left.at[(chunks - 1) % 2], right[chunks - 1], sum_ref)
+
+
+def near_kernel(src_ref, own_ref, mid_ref, sum_ref, pot_ref, wide, near_feat, *work):
+    feat, right, far_feat, left, flow, rows_ref = work
+    set_targets(own_ref, mid_ref, wide, near_feat, rows_ref)
+    set_sources(src_ref, mid_ref, feat, right, far_feat, own_ref.shape[1])
     sum_ref[...] = jnp.zeros(sum_ref.shape, f32)
     pot_ref[...] = jnp.zeros(pot_ref.shape, f32)
-    first = lax.axis_index("ia")
-    turn = [lax.rem(first + k, chunks) for k in range(chunks)]
-    for k in range(chunks):
-        pair_chunk(src_ref, pl.multiple_of(turn[k] * width, LANES), wide, left.at[k % 2], pot_ref, k == 0)
-        if k:
-            add_chunk(left.at[(k - 1) % 2], right[turn[k - 1]], sum_ref)
-    add_chunk(left.at[(chunks - 1) % 2], right[turn[chunks - 1]], sum_ref)
-
-
-def remote_kernel(*refs):
-    count = len(refs) - 8
-    sources = refs[:count]
-    own_ref, sum_in, pot_in, out_ref, feat, right, wide, left = refs[count:]
-    pl.run_scoped(
-        lambda sum_ref, pot_ref: remote_body(
-            sources, own_ref, sum_in, pot_in, out_ref, feat, right, wide, left, sum_ref, pot_ref
-        ),
-        pltpu.VMEM(sum_in.shape, f32),
-        pltpu.VMEM(pot_in.shape, f32),
-    )
-
-
-def remote_body(sources, own_ref, sum_in, pot_in, out_ref, feat, right, wide, left, sum_ref, pot_ref):
-    width = own_ref.shape[1]
-    chunks = right.shape[0]
-    spread_targets(own_ref, wide)
-    clear_features(feat)
+    pair_block(src_ref, wide, near_feat, sum_ref, pot_ref, right, far_feat, left, flow, True)
+
+
+def twin_kernel(count, *refs):
+    blocks = refs[:count]
+    src_ref, mid_ref, wide, near_feat, sum_in, pot_in = refs[count : count + 6]
+    sum_ref, pot_ref, other_sum, other_pot, other_own, other_wide, other_feat = refs[count + 6 : count + 13]
+    feat, right, far_feat, left, flow, rows_ref = refs[count + 13 :]
+    width = wide.shape[1]
+    stars = src_ref.shape[1]
+    mine = pl.ds(pl.multiple_of(lax.axis_index("ia") * width, LANES), width)
+    other_own[0:8, :] = blocks[-1][:, mine]
+    other_own[8:16, :] = blocks[-1][:, stars : stars + width]
+    set_targets(other_own, mid_ref, other_wide, other_feat, rows_ref)
     sum_ref[...] = sum_in[...]
     pot_ref[...] = pot_in[...]
-    for source in sources:
-        source_features(source, feat, right, width)
-        pair_chunk(source, 0, wide, left.at[0], pot_ref, False)
-
-        def two(i, unused):
-            pair_chunk(source, pl.multiple_of((2 * i + 1) * width, LANES), wide, left.at[1], pot_ref, False)
-            add_chunk(left.at[0], right[2 * i], sum_ref)
-            pair_chunk(source, pl.multiple_of((2 * i + 2) * width, LANES), wide, left.at[0], pot_ref, False)
-            add_chunk(left.at[1], right[2 * i + 1], sum_ref)
-            return 0
-
-        lax.fori_loop(0, (chunks - 2) // 2, two, 0)
-        pair_chunk(source, (chunks - 1) * width, wide, left.at[1], pot_ref, False)
-        add_chunk(left.at[0], right[chunks - 2], sum_ref)
-        add_chunk(left.at[1], right[chunks - 1], sum_ref)
+    other_sum[...] = jnp.zeros(other_sum.shape, f32)
+    other_pot[...] = jnp.zeros(other_pot.shape, f32)
+    for i, block in enumerate((*blocks, src_ref)):
+        set_sources(block, mid_ref, feat, right, far_feat, width)
+        if i < count:
+            pair_block(block, wide, near_feat, sum_ref, pot_ref, right, far_feat, left, flow, False)
+        pair_block(
+            block, other_wide, other_feat, other_sum, other_pot, right, far_feat, left, flow, i == count - 1
+        )
+
+
+def finish(own_ref, mid_ref, sum_ref, pot_ref, out_ref, cs):
+    width = own_ref.shape[1]
     sums = jnp.transpose(sum_ref[...])
     pot = jnp.sum(jnp.transpose(pot_ref[...]), axis=0, keepdims=True)
-    pos = own_ref[0:3, :]
-    vel = own_ref[3:6, :]
+    near_pos, near_vel = centred(own_ref[0:6, :], mid_ref)
     total = sums[18:19, :]
-    new_acc = (sums[0:3, :] - pos * total) + sums[3:6, :] + sums[6:9, :]
-    flow = (sums[9:12, :] - vel * total) + sums[12:15, :] + sums[15:18, :]
-    pull = (sums[32:35, :] - pos * sums[41:42, :]) + sums[35:38, :] + sums[38:41, :]
-    new_jolt = flow - 3.0 * pull
+    new_acc = (sums[0:3, :] - near_pos * total) + sums[3:6, :] + sums[6:9, :]
+    drift = (sums[9:12, :] - near_vel * total) + sums[12:15, :] + sums[15:18, :]
+    pull = (sums[32:35, :] - near_pos * sums[41:42, :]) + sums[35:38, :] + sums[38:41, :]
+    new_jolt = drift - 3.0 * pull
     position, velocity = correct(
-        pos, vel, own_ref[6:9, :], own_ref[9:12, :], own_ref[12:13, :], new_acc, new_jolt
+        own_ref[0:3, :], own_ref[3:6, :], own_ref[8:11, :], own_ref[11:14, :], own_ref[7:8, :], new_acc, new_jolt
     )
-    out_ref[0:3, :] = position
-    out_ref[3:6, :] = velocity
-    out_ref[6:8, :] = jnp.zeros((2, width), f32)
-    out_ref[8:11, :] = new_acc
-    out_ref[11:14, :] = new_jolt
-    out_ref[14:15, :] = -pot
-    out_ref[15:16, :] = jnp.zeros((1, width), f32)
+    out_ref[0:3, cs] = position
+    out_ref[3:6, cs] = velocity
+    out_ref[6:8, cs] = jnp.zeros((2, width), f32)
+    out_ref[8:11, cs] = new_acc
+    out_ref[11:14, cs] = new_jolt
+    out_ref[14:15, cs] = -pot
+    out_ref[15:16, cs] = jnp.zeros((1, width), f32)
+
+
+def last_kernel(count, *refs):
+    blocks = refs[:count]
+    mid_ref = refs[count]
+    sets = (refs[count + 1 : count + 6], refs[count + 6 : count + 11])
+    out_ref = refs[count + 11]
+    totals = (refs[count + 12 : count + 14], refs[count + 14 : count + 16])
+    feat, right, far_feat, left, flow, rows_ref = refs[count + 16 :]
+    for (own_ref, wide, near_feat, sum_in, pot_in), (sum_ref, pot_ref) in zip(sets, totals):
+        sum_ref[...] = sum_in[...]
+        pot_ref[...] = pot_in[...]
+    width = sets[0][0].shape[1]
+    for block in blocks:
+        set_sources(block, mid_ref, feat, right, far_feat, width)
+        for (own_ref, wide, near_feat, sum_in, pot_in), (sum_ref, pot_ref) in zip(sets, totals):
+            pair_block(block, wide, near_feat, sum_ref, pot_ref, right, far_feat, left, flow, False)
+    for i, ((own_ref, wide, near_feat, sum_in, pot_in), (sum_ref, pot_ref)) in enumerate(zip(sets, totals)):
+        finish(own_ref, mid_ref, sum_ref, pot_ref, out_ref, slice(i * width, i * width + width))
 
 
 def pick_kernel(ia_bits, ja_bits, width, first_slot, last, refs):
@@ -279,10 +335,12 @@
         local = local_ref[cs].reshape(1, LANES)
         apart_ja = lax.bitwise_xor(owner_ref[cs].reshape(1, LANES), my_ja)
         apart_ia = lax.bitwise_xor(local // width, my_ia)
-        flips = apart_ia + (apart_ja != 0).astype(jnp.int32)
+        step = lax.bitwise_and(apart_ja, (1 << (ja_bits - 1)) - 1)
+        flips = apart_ia + (step != 0).astype(jnp.int32)
         for i in range(1, ia_bits):
             flips = flips + lax.shift_right_logical(apart_ia, i)
-        slot = apart_ja + lax.shift_left(lax.shift_right_logical(apart_ia, 1), ja_bits)
+        slot = step + step + lax.shift_right_logical(apart_ja, ja_bits - 1)
+        slot = slot + lax.shift_left(lax.shift_right_logical(apart_ia, 1), ja_bits)
         slot = slot + lax.shift_left(lax.bitwise_and(flips, 1), ja_bits + ia_bits - 1)
         within = lax.rem(local, width)
         piece = jnp.broadcast_to((slot - first_slot) * per + within // LANES, (8, LANES))
@@ -313,11 +371,12 @@
         pairs = [(j * ni + i, (j ^ dj) * ni + (i ^ di)) for j in range(nj) for i in range(ni)]
         return lax.ppermute(x, ("ja", "ia"), pairs)
 
-    src, own = pl.pallas_call(
+    twin = nj // 2
+    src, long, own, mid = pl.pallas_call(
         predict_kernel,
-        out_shape=(shape_of(8, stars), shape_of(16, width)),
+        out_shape=(shape_of(8, stars), shape_of(8, stars + width), shape_of(16, width), shape_of(8, LANES)),
         in_specs=[pl.BlockSpec(memory_space=pltpu.HBM)] * 4,
-        out_specs=(VMEM, VMEM),
+        out_specs=(VMEM,) * 4,
         scratch_shapes=[
             pltpu.VMEM((6, stars), f32),
             pltpu.VMEM((6, stars), f32),
@@ -328,33 +387,50 @@
         compiler_params=PARAMS,
         name="predict",
     )(*(pltpu.with_memory_space_constraint(x, pltpu.HBM) for x in (pos_vel, acc_jerk, mass[None, :], age[None, :])))
-    others = [exchange(src, d, 1) for d in range(1, nj)]
+    others = [exchange(long if d == twin else src, d, 1) for d in range(1, nj)]
     scratch = [
-        pltpu.VMEM((2, COLS, stars), f32),
+        pltpu.VMEM((3, COLS, stars), f32),
         pltpu.VMEM((chunks, COLS, 4 * width), bf16),
-        pltpu.VMEM((6, width, LANES), f32),
+        pltpu.VMEM((chunks, COLS, width), bf16),
         pltpu.VMEM((2, width, 4 * width), f32),
+        pltpu.VMEM((2, width, width), f32),
+        pltpu.VMEM((COLS, width), f32),
     ]
-    pairs_cost = pl.CostEstimate(flops=40 * width * stars, transcendentals=width * stars, bytes_accessed=400000)
-    sums, pot = pl.pallas_call(
-        local_kernel,
-        out_shape=(shape_of(width, COLS), shape_of(width, LANES)),
-        in_specs=[VMEM] * 2,
-        out_specs=(VMEM, VMEM),
-        scratch_shapes=scratch,
-        cost_estimate=pairs_cost,
-        compiler_params=PARAMS,
-        name="near",
-    )(src, own)
-    block = pl.pallas_call(
-        remote_kernel,
-        out_shape=shape_of(16, width),
-        in_specs=[VMEM] * (len(others) + 3),
-        out_specs=VMEM,
-        scratch_shapes=scratch,
-        compiler_params=PARAMS,
-        name="far",
-    )(*others, own, sums, pot)
+    held = (shape_of(width, COLS), shape_of(width, LANES))
+    aims = (shape_of(3, width, LANES), shape_of(width, COLS))
+
+    def call(kernel, name, blocks, out_shape, more, args):
+        single = not isinstance(out_shape, tuple)
+        return pl.pallas_call(
+            kernel,
+            out_shape=out_shape,
+            in_specs=[VMEM] * len(args),
+            out_specs=VMEM if single else (VMEM,) * len(out_shape),
+            scratch_shapes=more + scratch,
+            compiler_params=PARAMS,
+            cost_estimate=pl.CostEstimate(
+                flops=blocks * 40 * width * stars, transcendentals=blocks * width * stars, bytes_accessed=400000
+            ),
+            name=name,
+        )(*args)
+
+    sums, pot, wide, feat = call(near_kernel, "near", 1, held + aims, [], (src, own, mid))
+    sums, pot, other_sums, other_pot, other_own, other_wide, other_feat = call(
+        lambda *refs: twin_kernel(twin, *refs),
+        "twin",
+        2 * twin + 1,
+        held + held + (shape_of(16, width),) + aims,
+        [],
+        (*others[:twin], src, mid, wide, feat, sums, pot),
+    )
+    block = call(
+        lambda *refs: last_kernel(nj - 1 - twin, *refs),
+        "last",
+        2 * (nj - 1 - twin),
+        shape_of(16, 2 * width),
+        [pltpu.VMEM(x.shape, f32) for x in held + held],
+        (*others[twin:], mid, own, wide, feat, sums, pot, other_own, other_wide, other_feat, other_sums, other_pot),
+    )
     count = active_local.shape[0]
 
     def pick(table, first_slot, before, last=False):
@@ -368,17 +444,23 @@
             name="pick",
         )(table, active_local, active_owner, *before)
 
-    table = jnp.concatenate([block, *(exchange(block, d, 1) for d in range(1, nj))], axis=1)
-    slots = nj
-    fresh, first_slot, found = table, 0, ()
-    for step in [(1 << bit) + 1 for bit in range(1, ia_bits)] + [1]:
-        came = exchange(table, 0, step)
-        found = pick(fresh, first_slot, found)
-        fresh, first_slot = came, slots
-        if step != 1:
-            table = jnp.concatenate([table, came], axis=1)
-        slots *= 2
-    return tuple(pick(fresh, first_slot, found, True))
+    table = jnp.concatenate([block, *(exchange(block, d, 1) for d in range(1, twin))], axis=1)
+    half = 1 << (ja_bits + ia_bits - 1)
+    tables = [(0, table)]
+    came = [(half, exchange(table, 0, 1))]
+    for bit in range(1, ia_bits):
+        for slot, there in list(tables):
+            fresh = exchange(there, 0, (1 << bit) + 1)
+            new_slot = slot + (nj << (bit - 1))
+            tables.append((new_slot, fresh))
+            came.append((half + new_slot, exchange(fresh, 0, 1)))
+    order = [tables[0], came[0]]
+    for pair in zip(tables[1:], came[1:]):
+        order.extend(pair)
+    found = ()
+    for i, (slot, there) in enumerate(order):
+        found = pick(there, slot, found, i == len(order) - 1)
+    return found
 
 
 def solution(mesh):

time: 28.3 us -> 27.2 us (0.961)
  Pallas kernels: 8.1 us -> 12.9 us
  waiting for transfers between devices: 7.88 us -> 3.97 us
  starting transfers between devices: 11.4 us -> 9.39 us
    pallas_call x3 -> x4, Pallas kernels: 6.32 us -> 11 us  [the longest x3 10.1 us: call(): pl.pallas_call(kernel, out_shape=out_shape, in_specs=[VMEM] * len(args),...]
    ppermute x8 -> x7, waiting for transfers between devices: 7.88 us -> 3.97 us  [exchange(): return lax.ppermute(x, ('ja', 'ia'), pairs)]
    ppermute x8 -> x7, starting transfers between devices: 11.4 us -> 9.39 us  [exchange(): return lax.ppermute(x, ('ja', 'ia'), pairs)]
    pallas_call x3 -> x4, Pallas kernels: 1.78 us -> 1.92 us  [pick(): pl.pallas_call(lambda *refs: pick_kernel(ia_bits, ja_bits, width, first_s...]
  transfers between devices with their start and end apart: 8 -> 7, of which waited for: 5 -> 2; matrix products, arithmetic and copies ran while one was open for 0% -> 0% of each run, Pallas kernels for 8% -> 31%
where the time goes in v3:
time: 27.2 us; the launch traced here: 27 us
  Pallas kernels  12.9 us (47%)
  starting transfers between devices  9.39 us (35%)
  waiting for transfers between devices  3.97 us (15%)
  between operations  0.7 us (3%)
    pallas_call x3, Pallas kernels, call(): pl.pallas_call(kernel, out_shape=out_shape, in_specs=[VMEM] * len(args),...  10.1 us
    ppermute x7, starting transfers between devices, exchange(): return lax.ppermute(x, ('ja', 'ia'), pairs)  9.39 us
    ppermute x7, waiting for transfers between devices, exchange(): return lax.ppermute(x, ('ja', 'ia'), pairs)  3.97 us
    pallas_call x4, Pallas kernels, pick(): pl.pallas_call(lambda *refs: pick_kernel(ia_bits, ja_bits, width, first_s...  1.92 us
    pallas_call x1, Pallas kernels, all_stars(): pl.pallas_call(predict_kernel, out_shape=(shape_of(8, stars), shape_of(8,...  0.92 us
  transfers between devices with their start and end apart: 7, of which 2 were waited for; matrix products, arithmetic and copies ran while one was open for 0% of the time, Pallas kernels for 31%

profile of v3, /device:TPU:0, one launch (start us, length us, event | category | flops | bytes accessed | tf_op | source)
XLA Modules:
  0.0 27.0 jit_solution(4775455944768063331)
XLA Ops:
  0.6 0.9 %predict.1 = (f32[8,1024]{1,0:T(8,128)S(1)}, f32[8,1280]{1,0:T(8,128)S(1)}, f32[16,256]{1,0:T(8,128)S(1)}, f32[8,128]{1,0:T(8,128)S(1)}) custom-call(f32[6,1024]{1,0:T(8,128)} %pv_hbm.1, f32[6,1024]{1,0:T(8,128)} %aj_hbm.1, f32[1,1024]{1,0:T(1,128)} %bitcast.2, f32[1,1024]{1,0:T(1,128)} %bitcast.3), custom_call_target="tpu_custom_call" | custom-call | tf_op jit(solution)/shard_map/predict/pallas_call | solution.py:375
  1.6 3.6 %collective-permute-start.2 = (f32[8,1280]{1,0:T(8,128)S(1)}, f32[8,1280]{1,0:T(8,128)S(1)}, u32[]{:S(2)}, u32[]{:S(2)}) collective-permute-start(f32[8,1280]{1,0:T(8,128)S(1)} %get-tuple-element.28), channel_id=1, source_target_pairs={{0,9},{1,8},{2,11},{3,10},{4,13},{5,12},{6,15},{7,14},{8,1},{9,0},... | collective-permute-start | bytes 122888 | tf_op jit(solution)/shard_map/ppermute | solution.py:372
  5.1 1.9 %collective-permute-start.1 = (f32[8,1024]{1,0:T(8,128)S(1)}, f32[8,1024]{1,0:T(8,128)S(1)}, u32[]{:S(2)}, u32[]{:S(2)}) collective-permute-start(f32[8,1024]{1,0:T(8,128)S(1)} %get-tuple-element.23.src_ref.refs_2_), channel_id=1, source_target_pairs={{0,5},{1,4},{2,7},{3,6},{4,1},{5,0},{6,3},{7,2},{8,13},{9,12},{10,... | collective-permute-start | bytes 98312 | tf_op jit(solution)/shard_map/ppermute | solution.py:372
  7.0 0.0 collective-permute-start
  7.0 1.6 %near.1 = (f32[256,64]{1,0:T(8,128)S(1)}, f32[256,128]{1,0:T(8,128)S(1)}, f32[3,256,128]{2,1,0:T(8,128)S(1)}, f32[256,64]{1,0:T(8,128)S(1)}) custom-call(f32[8,1024]{1,0:T(8,128)S(1)} %get-tuple-element.23.src_ref.refs_2_, f32[16,256]{1,0:T(8,128)S(1)} %get-tuple-element.25.own_ref.refs_2_, f32[8,128]{1,0:T(8,128)S(1)} %get-tuple-element.24.mid_ref.refs_3_.refs_1_), custom_call_target="tpu_custom_call" | custom-call | flops 10485760 | bytes 400000 | tf_op jit(solution)/shard_map/near/pallas_call | solution.py:404
  8.6 0.0 collective-permute-done.1.refs_0_
  8.6 0.0 collective-permute-done.2.refs_1_
  8.6 5.9 %twin.1 = (f32[256,64]{1,0:T(8,128)S(1)}, f32[256,128]{1,0:T(8,128)S(1)}, f32[256,64]{1,0:T(8,128)S(1)}, f32[256,128]{1,0:T(8,128)S(1)}, f32[16,256]{1,0:T(8,128...) custom-call(f32[8,1024]{1,0:T(8,128)S(1)} %collective-permute-done.1.refs_0_, ...), custom_call_target="tpu_custom_call" | custom-call | flops 52428800 | bytes 400000 | tf_op jit(solution)/shard_map/twin/pallas_call | solution.py:404
  14.5 0.0 collective-permute-done.refs_0_
  14.5 2.6 %last.1 = f32[16,512]{1,0:T(8,128)S(1)} custom-call(f32[8,1024]{1,0:T(8,128)S(1)} %collective-permute-done.refs_0_, f32[8,128]{1,0:T(8,128)S(1)} %get-tuple-element.24.mid_ref.refs_3_.refs_1_, f32[16,256]{1,0:T(8,128)S(1)} %get-tuple-element.25.own_ref.refs_2_, f32[3,256,128]{2,1,0:T(8,128)S(1)} %get-tuple-element.26.refs_4_.refs_3_, ...), custom_call_target="tpu_custom_call" | custom-call | flops 20971520 | bytes 400000 | tf_op jit(solution)/shard_map/last/pallas_call | solution.py:404
  17.1 0.0 copy-start
  17.1 0.0 copy-start.1
  17.1 2.1 %collective-permute-start.3 = (f32[16,512]{1,0:T(8,128)S(1)}, f32[16,512]{1,0:T(8,128)S(1)}, u32[]{:S(2)}, u32[]{:S(2)}) collective-permute-start(f32[16,512]{1,0:T(8,128)S(1)} %last.1), channel_id=1, source_target_pairs={{0,5},{1,4},{2,7},{3,6},{4,1},{5,0},{6,3},{7,2},{8,13},{9,12},{10,... | collective-permute-start | bytes 98312 | tf_op jit(solution)/shard_map/ppermute | solution.py:372
  19.2 1.6 %collective-permute-done.3 = f32[16,512]{1,0:T(8,128)S(1)} collective-permute-done((f32[16,512]{1,0:T(8,128)S(1)}, f32[16,512]{1,0:T(8,128)S(1)}, u32[]{:S(2)}, u32[]{:S(2)}) %collective-permute-start.3) | collective-permute-done | bytes 32800 | tf_op jit(solution)/shard_map/ppermute | solution.py:372
  20.8 1.4 %collective-permute-start.4 = (f32[16,1024]{1,0:T(8,128)S(1)}, f32[16,1024]{1,0:T(8,128)S(1)}, u32[]{:S(2)}, u32[]{:S(2)}) collective-permute-start(f32[16,1024]{1,0:T(8,128)S(1)} %pad_maximum_fusion.refs_0_), channel_id=1, source_target_pairs={{0,3},{1,2},{2,1},{3,0},{4,7},{5,6},{6,5},{7,4},{8,11},{9,10},{10,... | collective-permute-start | bytes 196616 | tf_op jit(solution)/shard_map/ppermute | solution.py:372
  22.2 0.2 collective-permute-start.6
  22.4 2.3 %collective-permute-done.4.refs_0_ = f32[16,1024]{1,0:T(8,128)S(1)} collective-permute-done((f32[16,1024]{1,0:T(8,128)S(1)}, f32[16,1024]{1,0:T(8,128)S(1)}, u32[]{:S(2)}, u32[]{:S(2)}) %collective-permute-start.4) | collective-permute-done | bytes 65568 | tf_op jit(solution)/shard_map/ppermute | solution.py:372
  24.8 0.3 collective-permute-start.5
  25.0 0.0 copy-done
  25.0 0.0 copy-done.1
  25.0 0.3 %pick.4 = (f32[8,1536]{1,0:T(8,128)S(1)}, f32[8,1536]{1,0:T(8,128)S(1)}) custom-call(f32[16,1024]{1,0:T(8,128)S(1)} %pad_maximum_fusion.refs_0_, s32[1536]{0:T(1024)S(1)} %copy-done, s32[1536]{0:T(1024)S(1)} %copy-done.1), custom_call_target="tpu_custom_call" | custom-call | flops 1572864 | bytes 400000 | tf_op jit(solution)/shard_map/pick/pallas_call | solution.py:437
  25.4 0.0 collective-permute-done.6.refs_0_
  25.4 0.3 %pick.5 = (f32[8,1536]{1,0:T(8,128)S(1)}, f32[8,1536]{1,0:T(8,128)S(1)}) custom-call(f32[16,1024]{1,0:T(8,128)S(1)} %collective-permute-done.6.refs_0_, s32[1536]{0:T(1024)S(1)} %copy-done, s32[1536]{0:T(1024)S(1)} %copy-done.1, f32[8,1536]{1,0:T(8,128)S(1)} %get-tuple-element.38.refs_3_, f32[8,1536]{1,0:T(8,128)S(1)} %get-tuple-element.39.refs_4_), custom_call_target="tpu_custom_call" | custom-call | flops 1572864 | bytes 400000 | tf_op jit(solution)/shard_map/pick/pallas_call | solution.py:437
  25.7 0.3 %pick.6 = (f32[8,1536]{1,0:T(8,128)S(1)}, f32[8,1536]{1,0:T(8,128)S(1)}) custom-call(f32[16,1024]{1,0:T(8,128)S(1)} %collective-permute-done.4.refs_0_, s32[1536]{0:T(1024)S(1)} %copy-done, s32[1536]{0:T(1024)S(1)} %copy-done.1, f32[8,1536]{1,0:T(8,128)S(1)} %get-tuple-element.40.refs_3_, f32[8,1536]{1,0:T(8,128)S(1)} %get-tuple-element.41.refs_4_), custom_call_target="tpu_custom_call" | custom-call | flops 1572864 | bytes 400000 | tf_op jit(solution)/shard_map/pick/pallas_call | solution.py:437
  26.0 0.0 collective-permute-done.5.refs_0_
  26.0 1.0 %pick.7 = (f32[6,1536]{1,0:T(8,128)}, f32[7,1536]{1,0:T(8,128)}) custom-call(f32[16,1024]{1,0:T(8,128)S(1)} %collective-permute-done.5.refs_0_, s32[1536]{0:T(1024)S(1)} %copy-done, s32[1536]{0:T(1024)S(1)} %copy-done.1, f32[8,1536]{1,0:T(8,128)S(1)} %get-tuple-element.42.refs_3_, f32[8,1536]{1,0:T(8,128)S(1)} %get-tuple-element.43.refs_4_), custom_call_target="tpu_custom_call" | custom-call | flops 1572864 | bytes 400000 | tf_op jit(solution)/shard_map/pick/pallas_call | solution.py:437
  (1 shorter events, 0.0 us)
Async XLA Ops:
  1.6 7.0 %collective-permute-start.2 = (f32[8,1280]{1,0:T(8,128)S(1)}, f32[8,1280]{1,0:T(8,128)S(1)}, u32[]{:S(2)}, u32[]{:S(2)}) collective-permute-start(f32[8,1280]{1,0:T(8,128)S(1)} %get-tuple-element.28), channel_id=1, source_target_pairs={{0,9},{1,8},{2,11},{3,10},{4,13},{5,12},{6,15},{7,14},{8,1},{9,0},... | collective-permute-start | bytes 122888 | tf_op jit(solution)/shard_map/ppermute | solution.py:372
  5.1 3.5 %collective-permute-start.1 = (f32[8,1024]{1,0:T(8,128)S(1)}, f32[8,1024]{1,0:T(8,128)S(1)}, u32[]{:S(2)}, u32[]{:S(2)}) collective-permute-start(f32[8,1024]{1,0:T(8,128)S(1)} %get-tuple-element.23.src_ref.refs_2_), channel_id=1, source_target_pairs={{0,5},{1,4},{2,7},{3,6},{4,1},{5,0},{6,3},{7,2},{8,13},{9,12},{10,... | collective-permute-start | bytes 98312 | tf_op jit(solution)/shard_map/ppermute | solution.py:372
  7.0 7.5 %collective-permute-start = (f32[8,1024]{1,0:T(8,128)S(1)}, f32[8,1024]{1,0:T(8,128)S(1)}, u32[]{:S(2)}, u32[]{:S(2)}) collective-permute-start(f32[8,1024]{1,0:T(8,128)S(1)} %get-tuple-element.23.src_ref.refs_2_), channel_id=1, source_target_pairs={{0,13},{1,12},{2,15},{3,14},{4,9},{5,8},{6,11},{7,10},{8,5},{9,4},... | collective-permute-start | bytes 98312 | tf_op jit(solution)/shard_map/ppermute | solution.py:372
  17.1 7.9 %copy-start = (s32[1536]{0:T(1024)S(1)}, s32[1536]{0:T(1024)}, u32[]{:S(2)}) copy-start(s32[1536]{0:T(1024)} %refs_1_.7) | copy-start | bytes 18436
  17.1 7.9 %copy-start.1 = (s32[1536]{0:T(1024)S(1)}, s32[1536]{0:T(1024)}, u32[]{:S(2)}) copy-start(s32[1536]{0:T(1024)} %refs_2_.7) | copy-start | bytes 18436
  17.1 3.7 %collective-permute-start.3 = (f32[16,512]{1,0:T(8,128)S(1)}, f32[16,512]{1,0:T(8,128)S(1)}, u32[]{:S(2)}, u32[]{:S(2)}) collective-permute-start(f32[16,512]{1,0:T(8,128)S(1)} %last.1), channel_id=1, source_target_pairs={{0,5},{1,4},{2,7},{3,6},{4,1},{5,0},{6,3},{7,2},{8,13},{9,12},{10,... | collective-permute-start | bytes 98312 | tf_op jit(solution)/shard_map/ppermute | solution.py:372
  20.8 3.9 %collective-permute-start.4 = (f32[16,1024]{1,0:T(8,128)S(1)}, f32[16,1024]{1,0:T(8,128)S(1)}, u32[]{:S(2)}, u32[]{:S(2)}) collective-permute-start(f32[16,1024]{1,0:T(8,128)S(1)} %pad_maximum_fusion.refs_0_), channel_id=1, source_target_pairs={{0,3},{1,2},{2,1},{3,0},{4,7},{5,6},{6,5},{7,4},{8,11},{9,10},{10,... | collective-permute-start | bytes 196616 | tf_op jit(solution)/shard_map/ppermute | solution.py:372
  22.2 3.2 %collective-permute-start.6 = (f32[16,1024]{1,0:T(8,128)S(1)}, f32[16,1024]{1,0:T(8,128)S(1)}, u32[]{:S(2)}, u32[]{:S(2)}) collective-permute-start(f32[16,1024]{1,0:T(8,128)S(1)} %pad_maximum_fusion.refs_0_), channel_id=1, source_target_pairs={{0,1},{1,0},{2,3},{3,2},{4,5},{5,4},{6,7},{7,6},{8,9},{9,8},{10,11... | collective-permute-start | bytes 196616 | tf_op jit(solution)/shard_map/ppermute | solution.py:372
  24.8 1.3 %collective-permute-start.5 = (f32[16,1024]{1,0:T(8,128)S(1)}, f32[16,1024]{1,0:T(8,128)S(1)}, u32[]{:S(2)}, u32[]{:S(2)}) collective-permute-start(f32[16,1024]{1,0:T(8,128)S(1)} %collective-permute-done.4.refs_0_), channel_id=1, source_target_pairs={{0,1},{1,0},{2,3},{3,2},{4,5},{5,4},{6,7},{7,6},{8,9},{9,8},{10,11... | collective-permute-start | bytes 196616 | tf_op jit(solution)/shard_map/ppermute | solution.py:372

commit v4 on v3

--- a/solution.py
+++ b/solution.py
@@ -10,7 +10,7 @@
 bf16 = jnp.bfloat16
 LANES = 128
 ROWS = 16
-COLS = 64
+COLS = 48
 VMEM = pl.BlockSpec(memory_space=pltpu.VMEM)
 PARAMS = pltpu.CompilerParams(vmem_limit_bytes=16 << 20)
 BOTH_MINOR = (((1,), (1,)), ((), ()))
@@ -146,19 +146,27 @@
     return three_parts(jnp.sum(a * b, axis=0, keepdims=True))
 
 
+def set_constants(feat, rows_ref):
+    feat[...] = jnp.zeros(feat.shape, f32)
+    rows_ref[...] = jnp.zeros(rows_ref.shape, f32)
+    one = jnp.ones((3, feat.shape[2]), f32)
+    feat[0, 18:19, :] = one[0:1, :]
+    feat[1, 33:34, :] = one[0:1, :]
+    feat[2, 39:42, :] = one
+    rows_ref[36:39, :] = one[:, 0 : rows_ref.shape[1]]
+
+
 def set_targets(own_ref, mid_ref, wide, near_feat, rows_ref):
     width = own_ref.shape[1]
     turned = jnp.transpose(own_ref[0:8, :])
     for c in range(3):
         wide[c] = jnp.broadcast_to(turned[:, c : c + 1], (width, LANES))
     pos, vel = centred(own_ref[0:6, :], mid_ref)
-    rows_ref[...] = jnp.zeros(rows_ref.shape, f32)
     row = 0
     for high, mid, low in (three_parts(-vel), three_parts(-pos)):
         for x in (high, high, mid, high, mid, low):
             rows_ref[row : row + 3, :] = x
             row += 3
-    rows_ref[row : row + 3, :] = jnp.ones((3, width), f32)
     for i, x in enumerate(dot_parts(pos, vel)):
         rows_ref[row + 3 + i : row + 4 + i, :] = x
     near_feat[...] = jnp.transpose(rows_ref[...])
@@ -169,14 +177,10 @@
     pos, vel = centred(src_ref[0:6, 0:count], mid_ref)
     pos_parts = three_parts(pos)
     vel_parts = three_parts(vel)
-    one = jnp.ones((3, count), f32)
-    feat[...] = jnp.zeros(feat.shape, f32)
     for i, x in enumerate((*pos_parts, *vel_parts)):
         feat[0, 3 * i : 3 * i + 3, :] = x
-    feat[0, 18:19, :] = one[0:1, :]
     for i, x in enumerate(pos_parts):
-        feat[1, 32 + 3 * i : 35 + 3 * i, :] = x
-    feat[1, 41:42, :] = one[0:1, :]
+        feat[1, 24 + 3 * i : 27 + 3 * i, :] = x
     row = 0
     for high, mid, low in (pos_parts, vel_parts):
         for x in (high, mid, high, low, mid, high):
@@ -184,7 +188,6 @@
             row += 3
     for i, x in enumerate(dot_parts(pos, vel)):
         feat[2, row + i : row + i + 1, :] = x
-    feat[2, row + 3 : row + 6, :] = one
     for k in range(right.shape[0]):
         cs = slice(k * width, k * width + width)
         for i in range(4):
@@ -194,19 +197,16 @@
 
 def pair_chunk(source, offset, flow, wide, left, pot_ref, shift):
     width = wide.shape[1]
-    for rb in range(width // ROWS):
-        rs = slice(rb * ROWS, rb * ROWS + ROWS)
-        target = [wide[c, rs, :] for c in range(3)]
-        pot = pot_ref[rs, :]
-        for j in range(width // LANES):
-            cs = slice(offset + LANES * j, offset + LANES * j + LANES)
-            dx, dy, dz = (
-                jnp.broadcast_to(source[c : c + 1, cs], (ROWS, LANES)) - target[c] for c in range(3)
-            )
+    for j in range(width // LANES):
+        cs = slice(offset + LANES * j, offset + LANES * j + LANES)
+        source_rows = [jnp.broadcast_to(source[c : c + 1, cs], (ROWS, LANES)) for c in (0, 1, 2, 6)]
+        for rb in range(width // ROWS):
+            rs = slice(rb * ROWS, rb * ROWS + ROWS)
+            dx, dy, dz = (source_rows[c] - wide[c, rs, :] for c in range(3))
             inverse = lax.rsqrt(((dx * dx + soften) + dy * dy) + dz * dz)
             inv_sq = inverse * inverse
-            weighted = jnp.broadcast_to(source[6:7, cs], (ROWS, LANES)) * inverse
-            pot = pot + weighted
+            weighted = source_rows[3] * inverse
+            pot_ref[rs, :] += weighted
             cube = weighted * inv_sq
             if shift is not None and rb * ROWS // LANES == j:
                 here = lax.broadcasted_iota(jnp.int32, (ROWS, LANES), 0) + (rb * ROWS - j * LANES + shift)
@@ -221,7 +221,6 @@
             )
             for i, x in enumerate(parts):
                 left[rs, i * width + LANES * j : i * width + LANES * j + LANES] = x
-        pot_ref[rs, :] = pot
 
 
 def add_chunk(left, right, sum_ref):
@@ -250,6 +249,7 @@
 
 def near_kernel(src_ref, own_ref, mid_ref, sum_ref, pot_ref, wide, near_feat, *work):
     feat, right, far_feat, left, flow, rows_ref = work
+    set_constants(feat, rows_ref)
     set_targets(own_ref, mid_ref, wide, near_feat, rows_ref)
     set_sources(src_ref, mid_ref, feat, right, far_feat, own_ref.shape[1])
     sum_ref[...] = jnp.zeros(sum_ref.shape, f32)
@@ -267,6 +267,7 @@
     mine = pl.ds(pl.multiple_of(lax.axis_index("ia") * width, LANES), width)
     other_own[0:8, :] = blocks[-1][:, mine]
     other_own[8:16, :] = blocks[-1][:, stars : stars + width]
+    set_constants(feat, rows_ref)
     set_targets(other_own, mid_ref, other_wide, other_feat, rows_ref)
     sum_ref[...] = sum_in[...]
     pot_ref[...] = pot_in[...]
@@ -289,7 +290,7 @@
     total = sums[18:19, :]
     new_acc = (sums[0:3, :] - near_pos * total) + sums[3:6, :] + sums[6:9, :]
     drift = (sums[9:12, :] - near_vel * total) + sums[12:15, :] + sums[15:18, :]
-    pull = (sums[32:35, :] - near_pos * sums[41:42, :]) + sums[35:38, :] + sums[38:41, :]
+    pull = (sums[24:27, :] - near_pos * sums[33:34, :]) + sums[27:30, :] + sums[30:33, :]
     new_jolt = drift - 3.0 * pull
     position, velocity = correct(
         own_ref[0:3, :], own_ref[3:6, :], own_ref[8:11, :], own_ref[11:14, :], own_ref[7:8, :], new_acc, new_jolt
@@ -310,6 +311,7 @@
     out_ref = refs[count + 11]
     totals = (refs[count + 12 : count + 14], refs[count + 14 : count + 16])
     feat, right, far_feat, left, flow, rows_ref = refs[count + 16 :]
+    set_constants(feat, rows_ref)
     for (own_ref, wide, near_feat, sum_in, pot_in), (sum_ref, pot_ref) in zip(sets, totals):
         sum_ref[...] = sum_in[...]
         pot_ref[...] = pot_in[...]

time: 27.2 us -> 27 us (level)
  no operation moved by 1% of the time
where the time goes in v4:
time: 27 us; the launch traced here: 26.8 us
  Pallas kernels  12.8 us (47%)
  starting transfers between devices  9.39 us (35%)
  waiting for transfers between devices  3.97 us (15%)
  between operations  0.7 us (3%)
    pallas_call x3, Pallas kernels, call(): pl.pallas_call(kernel, out_shape=out_shape, in_specs=[VMEM] * len(args),...  9.92 us
    ppermute x7, starting transfers between devices, exchange(): return lax.ppermute(x, ('ja', 'ia'), pairs)  9.39 us
    ppermute x7, waiting for transfers between devices, exchange(): return lax.ppermute(x, ('ja', 'ia'), pairs)  3.97 us
    pallas_call x4, Pallas kernels, pick(): pl.pallas_call(lambda *refs: pick_kernel(ia_bits, ja_bits, width, first_s...  1.92 us
    pallas_call x1, Pallas kernels, all_stars(): pl.pallas_call(predict_kernel, out_shape=(shape_of(8, stars), shape_of(8,...  0.92 us
  transfers between devices with their start and end apart: 7, of which 2 were waited for; matrix products, arithmetic and copies ran while one was open for 0% of the time, Pallas kernels for 31%

profile of v4, /device:TPU:0, one launch (start us, length us, event | category | flops | bytes accessed | tf_op | source)
XLA Modules:
  0.0 26.8 jit_solution(10391952397955917897)
XLA Ops:
  0.6 0.9 %predict.1 = (f32[8,1024]{1,0:T(8,128)S(1)}, f32[8,1280]{1,0:T(8,128)S(1)}, f32[16,256]{1,0:T(8,128)S(1)}, f32[8,128]{1,0:T(8,128)S(1)}) custom-call(f32[6,1024]{1,0:T(8,128)} %pv_hbm.1, f32[6,1024]{1,0:T(8,128)} %aj_hbm.1, f32[1,1024]{1,0:T(1,128)} %bitcast.2, f32[1,1024]{1,0:T(1,128)} %bitcast.3), custom_call_target="tpu_custom_call" | custom-call | tf_op jit(solution)/shard_map/predict/pallas_call | solution.py:377
  1.6 3.6 %collective-permute-start.2 = (f32[8,1280]{1,0:T(8,128)S(1)}, f32[8,1280]{1,0:T(8,128)S(1)}, u32[]{:S(2)}, u32[]{:S(2)}) collective-permute-start(f32[8,1280]{1,0:T(8,128)S(1)} %get-tuple-element.28), channel_id=1, source_target_pairs={{0,9},{1,8},{2,11},{3,10},{4,13},{5,12},{6,15},{7,14},{8,1},{9,0},... | collective-permute-start | bytes 122888 | tf_op jit(solution)/shard_map/ppermute | solution.py:374
  5.1 1.9 %collective-permute-start.1 = (f32[8,1024]{1,0:T(8,128)S(1)}, f32[8,1024]{1,0:T(8,128)S(1)}, u32[]{:S(2)}, u32[]{:S(2)}) collective-permute-start(f32[8,1024]{1,0:T(8,128)S(1)} %get-tuple-element.23.src_ref.refs_2_), channel_id=1, source_target_pairs={{0,5},{1,4},{2,7},{3,6},{4,1},{5,0},{6,3},{7,2},{8,13},{9,12},{10,... | collective-permute-start | bytes 98312 | tf_op jit(solution)/shard_map/ppermute | solution.py:374
  7.0 0.0 collective-permute-start
  7.0 1.6 %near.1 = (f32[256,48]{1,0:T(8,128)S(1)}, f32[256,128]{1,0:T(8,128)S(1)}, f32[3,256,128]{2,1,0:T(8,128)S(1)}, f32[256,48]{1,0:T(8,128)S(1)}) custom-call(f32[8,1024]{1,0:T(8,128)S(1)} %get-tuple-element.23.src_ref.refs_2_, f32[16,256]{1,0:T(8,128)S(1)} %get-tuple-element.25.own_ref.refs_2_, f32[8,128]{1,0:T(8,128)S(1)} %get-tuple-element.24.mid_ref.refs_3_.refs_1_), custom_call_target="tpu_custom_call" | custom-call | flops 10485760 | bytes 400000 | tf_op jit(solution)/shard_map/near/pallas_call | solution.py:406
  8.6 0.0 collective-permute-done.1.refs_0_
  8.6 0.0 collective-permute-done.2.refs_1_
  8.6 5.8 %twin.1 = (f32[256,48]{1,0:T(8,128)S(1)}, f32[256,128]{1,0:T(8,128)S(1)}, f32[256,48]{1,0:T(8,128)S(1)}, f32[256,128]{1,0:T(8,128)S(1)}, f32[16,256]{1,0:T(8,128...) custom-call(f32[8,1024]{1,0:T(8,128)S(1)} %collective-permute-done.1.refs_0_, ...), custom_call_target="tpu_custom_call" | custom-call | flops 52428800 | bytes 400000 | tf_op jit(solution)/shard_map/twin/pallas_call | solution.py:406
  14.4 0.0 collective-permute-done.refs_0_
  14.4 2.6 %last.1 = f32[16,512]{1,0:T(8,128)S(1)} custom-call(f32[8,1024]{1,0:T(8,128)S(1)} %collective-permute-done.refs_0_, f32[8,128]{1,0:T(8,128)S(1)} %get-tuple-element.24.mid_ref.refs_3_.refs_1_, f32[16,256]{1,0:T(8,128)S(1)} %get-tuple-element.25.own_ref.refs_2_, f32[3,256,128]{2,1,0:T(8,128)S(1)} %get-tuple-element.26.refs_4_.refs_3_, ...), custom_call_target="tpu_custom_call" | custom-call | flops 20971520 | bytes 400000 | tf_op jit(solution)/shard_map/last/pallas_call | solution.py:406
  17.0 0.0 copy-start
  17.0 0.0 copy-start.1
  17.0 2.1 %collective-permute-start.3 = (f32[16,512]{1,0:T(8,128)S(1)}, f32[16,512]{1,0:T(8,128)S(1)}, u32[]{:S(2)}, u32[]{:S(2)}) collective-permute-start(f32[16,512]{1,0:T(8,128)S(1)} %last.1), channel_id=1, source_target_pairs={{0,5},{1,4},{2,7},{3,6},{4,1},{5,0},{6,3},{7,2},{8,13},{9,12},{10,... | collective-permute-start | bytes 98312 | tf_op jit(solution)/shard_map/ppermute | solution.py:374
  19.1 1.6 %collective-permute-done.3 = f32[16,512]{1,0:T(8,128)S(1)} collective-permute-done((f32[16,512]{1,0:T(8,128)S(1)}, f32[16,512]{1,0:T(8,128)S(1)}, u32[]{:S(2)}, u32[]{:S(2)}) %collective-permute-start.3) | collective-permute-done | bytes 32800 | tf_op jit(solution)/shard_map/ppermute | solution.py:374
  20.7 1.4 %collective-permute-start.4 = (f32[16,1024]{1,0:T(8,128)S(1)}, f32[16,1024]{1,0:T(8,128)S(1)}, u32[]{:S(2)}, u32[]{:S(2)}) collective-permute-start(f32[16,1024]{1,0:T(8,128)S(1)} %pad_maximum_fusion.refs_0_), channel_id=1, source_target_pairs={{0,3},{1,2},{2,1},{3,0},{4,7},{5,6},{6,5},{7,4},{8,11},{9,10},{10,... | collective-permute-start | bytes 196616 | tf_op jit(solution)/shard_map/ppermute | solution.py:374
  22.0 0.2 collective-permute-start.6
  22.3 2.3 %collective-permute-done.4.refs_0_ = f32[16,1024]{1,0:T(8,128)S(1)} collective-permute-done((f32[16,1024]{1,0:T(8,128)S(1)}, f32[16,1024]{1,0:T(8,128)S(1)}, u32[]{:S(2)}, u32[]{:S(2)}) %collective-permute-start.4) | collective-permute-done | bytes 65568 | tf_op jit(solution)/shard_map/ppermute | solution.py:374
  24.6 0.3 collective-permute-start.5
  24.9 0.0 copy-done
  24.9 0.0 copy-done.1
  24.9 0.3 %pick.4 = (f32[8,1536]{1,0:T(8,128)S(1)}, f32[8,1536]{1,0:T(8,128)S(1)}) custom-call(f32[16,1024]{1,0:T(8,128)S(1)} %pad_maximum_fusion.refs_0_, s32[1536]{0:T(1024)S(1)} %copy-done, s32[1536]{0:T(1024)S(1)} %copy-done.1), custom_call_target="tpu_custom_call" | custom-call | flops 1572864 | bytes 400000 | tf_op jit(solution)/shard_map/pick/pallas_call | solution.py:439
  25.2 0.0 collective-permute-done.6.refs_0_
  25.2 0.3 %pick.5 = (f32[8,1536]{1,0:T(8,128)S(1)}, f32[8,1536]{1,0:T(8,128)S(1)}) custom-call(f32[16,1024]{1,0:T(8,128)S(1)} %collective-permute-done.6.refs_0_, s32[1536]{0:T(1024)S(1)} %copy-done, s32[1536]{0:T(1024)S(1)} %copy-done.1, f32[8,1536]{1,0:T(8,128)S(1)} %get-tuple-element.38.refs_3_, f32[8,1536]{1,0:T(8,128)S(1)} %get-tuple-element.39.refs_4_), custom_call_target="tpu_custom_call" | custom-call | flops 1572864 | bytes 400000 | tf_op jit(solution)/shard_map/pick/pallas_call | solution.py:439
  25.6 0.3 %pick.6 = (f32[8,1536]{1,0:T(8,128)S(1)}, f32[8,1536]{1,0:T(8,128)S(1)}) custom-call(f32[16,1024]{1,0:T(8,128)S(1)} %collective-permute-done.4.refs_0_, s32[1536]{0:T(1024)S(1)} %copy-done, s32[1536]{0:T(1024)S(1)} %copy-done.1, f32[8,1536]{1,0:T(8,128)S(1)} %get-tuple-element.40.refs_3_, f32[8,1536]{1,0:T(8,128)S(1)} %get-tuple-element.41.refs_4_), custom_call_target="tpu_custom_call" | custom-call | flops 1572864 | bytes 400000 | tf_op jit(solution)/shard_map/pick/pallas_call | solution.py:439
  25.9 0.0 collective-permute-done.5.refs_0_
  25.9 1.0 %pick.7 = (f32[6,1536]{1,0:T(8,128)}, f32[7,1536]{1,0:T(8,128)}) custom-call(f32[16,1024]{1,0:T(8,128)S(1)} %collective-permute-done.5.refs_0_, s32[1536]{0:T(1024)S(1)} %copy-done, s32[1536]{0:T(1024)S(1)} %copy-done.1, f32[8,1536]{1,0:T(8,128)S(1)} %get-tuple-element.42.refs_3_, f32[8,1536]{1,0:T(8,128)S(1)} %get-tuple-element.43.refs_4_), custom_call_target="tpu_custom_call" | custom-call | flops 1572864 | bytes 400000 | tf_op jit(solution)/shard_map/pick/pallas_call | solution.py:439
  (1 shorter events, 0.0 us)
Async XLA Ops:
  1.6 7.0 %collective-permute-start.2 = (f32[8,1280]{1,0:T(8,128)S(1)}, f32[8,1280]{1,0:T(8,128)S(1)}, u32[]{:S(2)}, u32[]{:S(2)}) collective-permute-start(f32[8,1280]{1,0:T(8,128)S(1)} %get-tuple-element.28), channel_id=1, source_target_pairs={{0,9},{1,8},{2,11},{3,10},{4,13},{5,12},{6,15},{7,14},{8,1},{9,0},... | collective-permute-start | bytes 122888 | tf_op jit(solution)/shard_map/ppermute | solution.py:374
  5.1 3.5 %collective-permute-start.1 = (f32[8,1024]{1,0:T(8,128)S(1)}, f32[8,1024]{1,0:T(8,128)S(1)}, u32[]{:S(2)}, u32[]{:S(2)}) collective-permute-start(f32[8,1024]{1,0:T(8,128)S(1)} %get-tuple-element.23.src_ref.refs_2_), channel_id=1, source_target_pairs={{0,5},{1,4},{2,7},{3,6},{4,1},{5,0},{6,3},{7,2},{8,13},{9,12},{10,... | collective-permute-start | bytes 98312 | tf_op jit(solution)/shard_map/ppermute | solution.py:374
  7.0 7.4 %collective-permute-start = (f32[8,1024]{1,0:T(8,128)S(1)}, f32[8,1024]{1,0:T(8,128)S(1)}, u32[]{:S(2)}, u32[]{:S(2)}) collective-permute-start(f32[8,1024]{1,0:T(8,128)S(1)} %get-tuple-element.23.src_ref.refs_2_), channel_id=1, source_target_pairs={{0,13},{1,12},{2,15},{3,14},{4,9},{5,8},{6,11},{7,10},{8,5},{9,4},... | collective-permute-start | bytes 98312 | tf_op jit(solution)/shard_map/ppermute | solution.py:374
  17.0 7.9 %copy-start = (s32[1536]{0:T(1024)S(1)}, s32[1536]{0:T(1024)}, u32[]{:S(2)}) copy-start(s32[1536]{0:T(1024)} %refs_1_.7) | copy-start | bytes 18436
  17.0 7.9 %copy-start.1 = (s32[1536]{0:T(1024)S(1)}, s32[1536]{0:T(1024)}, u32[]{:S(2)}) copy-start(s32[1536]{0:T(1024)} %refs_2_.7) | copy-start | bytes 18436
  17.0 3.7 %collective-permute-start.3 = (f32[16,512]{1,0:T(8,128)S(1)}, f32[16,512]{1,0:T(8,128)S(1)}, u32[]{:S(2)}, u32[]{:S(2)}) collective-permute-start(f32[16,512]{1,0:T(8,128)S(1)} %last.1), channel_id=1, source_target_pairs={{0,5},{1,4},{2,7},{3,6},{4,1},{5,0},{6,3},{7,2},{8,13},{9,12},{10,... | collective-permute-start | bytes 98312 | tf_op jit(solution)/shard_map/ppermute | solution.py:374
  20.7 3.9 %collective-permute-start.4 = (f32[16,1024]{1,0:T(8,128)S(1)}, f32[16,1024]{1,0:T(8,128)S(1)}, u32[]{:S(2)}, u32[]{:S(2)}) collective-permute-start(f32[16,1024]{1,0:T(8,128)S(1)} %pad_maximum_fusion.refs_0_), channel_id=1, source_target_pairs={{0,3},{1,2},{2,1},{3,0},{4,7},{5,6},{6,5},{7,4},{8,11},{9,10},{10,... | collective-permute-start | bytes 196616 | tf_op jit(solution)/shard_map/ppermute | solution.py:374
  22.0 3.2 %collective-permute-start.6 = (f32[16,1024]{1,0:T(8,128)S(1)}, f32[16,1024]{1,0:T(8,128)S(1)}, u32[]{:S(2)}, u32[]{:S(2)}) collective-permute-start(f32[16,1024]{1,0:T(8,128)S(1)} %pad_maximum_fusion.refs_0_), channel_id=1, source_target_pairs={{0,1},{1,0},{2,3},{3,2},{4,5},{5,4},{6,7},{7,6},{8,9},{9,8},{10,11... | collective-permute-start | bytes 196616 | tf_op jit(solution)/shard_map/ppermute | solution.py:374
  24.6 1.3 %collective-permute-start.5 = (f32[16,1024]{1,0:T(8,128)S(1)}, f32[16,1024]{1,0:T(8,128)S(1)}, u32[]{:S(2)}, u32[]{:S(2)}) collective-permute-start(f32[16,1024]{1,0:T(8,128)S(1)} %collective-permute-done.4.refs_0_), channel_id=1, source_target_pairs={{0,1},{1,0},{2,3},{3,2},{4,5},{5,4},{6,7},{7,6},{8,9},{9,8},{10,11... | collective-permute-start | bytes 196616 | tf_op jit(solution)/shard_map/ppermute | solution.py:374

commit v5 on v4

--- a/solution.py
+++ b/solution.py
@@ -9,7 +9,7 @@
 f32 = jnp.float32
 bf16 = jnp.bfloat16
 LANES = 128
-ROWS = 16
+ROWS = 64
 COLS = 48
 VMEM = pl.BlockSpec(memory_space=pltpu.VMEM)
 PARAMS = pltpu.CompilerParams(vmem_limit_bytes=16 << 20)

time: 27 us -> 27 us (level)
  no operation moved by 1% of the time
where the time goes in v5:
time: 27 us; the launch traced here: 26.8 us
  Pallas kernels  12.7 us (47%)
  starting transfers between devices  9.42 us (35%)
  waiting for transfers between devices  3.94 us (15%)
  between operations  0.7 us (3%)
    pallas_call x3, Pallas kernels, call(): pl.pallas_call(kernel, out_shape=out_shape, in_specs=[VMEM] * len(args),...  9.89 us
    ppermute x7, starting transfers between devices, exchange(): return lax.ppermute(x, ('ja', 'ia'), pairs)  9.42 us
    ppermute x7, waiting for transfers between devices, exchange(): return lax.ppermute(x, ('ja', 'ia'), pairs)  3.94 us
    pallas_call x4, Pallas kernels, pick(): pl.pallas_call(lambda *refs: pick_kernel(ia_bits, ja_bits, width, first_s...  1.92 us
    pallas_call x1, Pallas kernels, all_stars(): pl.pallas_call(predict_kernel, out_shape=(shape_of(8, stars), shape_of(8,...  0.92 us
  transfers between devices with their start and end apart: 7, of which 2 were waited for; matrix products, arithmetic and copies ran while one was open for 0% of the time, Pallas kernels for 31%

profile of v5, /device:TPU:0, one launch (start us, length us, event | category | flops | bytes accessed | tf_op | source)
XLA Modules:
  0.0 26.8 jit_solution(9090480880764407371)
XLA Ops:
  0.6 0.9 %predict.1 = (f32[8,1024]{1,0:T(8,128)S(1)}, f32[8,1280]{1,0:T(8,128)S(1)}, f32[16,256]{1,0:T(8,128)S(1)}, f32[8,128]{1,0:T(8,128)S(1)}) custom-call(f32[6,1024]{1,0:T(8,128)} %pv_hbm.1, f32[6,1024]{1,0:T(8,128)} %aj_hbm.1, f32[1,1024]{1,0:T(1,128)} %bitcast.2, f32[1,1024]{1,0:T(1,128)} %bitcast.3), custom_call_target="tpu_custom_call" | custom-call | tf_op jit(solution)/shard_map/predict/pallas_call | solution.py:377
  1.6 3.6 %collective-permute-start.2 = (f32[8,1280]{1,0:T(8,128)S(1)}, f32[8,1280]{1,0:T(8,128)S(1)}, u32[]{:S(2)}, u32[]{:S(2)}) collective-permute-start(f32[8,1280]{1,0:T(8,128)S(1)} %get-tuple-element.28), channel_id=1, source_target_pairs={{0,9},{1,8},{2,11},{3,10},{4,13},{5,12},{6,15},{7,14},{8,1},{9,0},... | collective-permute-start | bytes 122888 | tf_op jit(solution)/shard_map/ppermute | solution.py:374
  5.1 1.9 %collective-permute-start.1 = (f32[8,1024]{1,0:T(8,128)S(1)}, f32[8,1024]{1,0:T(8,128)S(1)}, u32[]{:S(2)}, u32[]{:S(2)}) collective-permute-start(f32[8,1024]{1,0:T(8,128)S(1)} %get-tuple-element.23.src_ref.refs_2_), channel_id=1, source_target_pairs={{0,5},{1,4},{2,7},{3,6},{4,1},{5,0},{6,3},{7,2},{8,13},{9,12},{10,... | collective-permute-start | bytes 98312 | tf_op jit(solution)/shard_map/ppermute | solution.py:374
  7.0 0.0 collective-permute-start
  7.0 1.6 %near.1 = (f32[256,48]{1,0:T(8,128)S(1)}, f32[256,128]{1,0:T(8,128)S(1)}, f32[3,256,128]{2,1,0:T(8,128)S(1)}, f32[256,48]{1,0:T(8,128)S(1)}) custom-call(f32[8,1024]{1,0:T(8,128)S(1)} %get-tuple-element.23.src_ref.refs_2_, f32[16,256]{1,0:T(8,128)S(1)} %get-tuple-element.25.own_ref.refs_2_, f32[8,128]{1,0:T(8,128)S(1)} %get-tuple-element.24.mid_ref.refs_3_.refs_1_), custom_call_target="tpu_custom_call" | custom-call | flops 10485760 | bytes 400000 | tf_op jit(solution)/shard_map/near/pallas_call | solution.py:406
  8.6 0.0 collective-permute-done.1.refs_0_
  8.6 0.0 collective-permute-done.2.refs_1_
  8.6 5.7 %twin.1 = (f32[256,48]{1,0:T(8,128)S(1)}, f32[256,128]{1,0:T(8,128)S(1)}, f32[256,48]{1,0:T(8,128)S(1)}, f32[256,128]{1,0:T(8,128)S(1)}, f32[16,256]{1,0:T(8,128...) custom-call(f32[8,1024]{1,0:T(8,128)S(1)} %collective-permute-done.1.refs_0_, ...), custom_call_target="tpu_custom_call" | custom-call | flops 52428800 | bytes 400000 | tf_op jit(solution)/shard_map/twin/pallas_call | solution.py:406
  14.3 0.0 collective-permute-done.refs_0_
  14.3 2.6 %last.1 = f32[16,512]{1,0:T(8,128)S(1)} custom-call(f32[8,1024]{1,0:T(8,128)S(1)} %collective-permute-done.refs_0_, f32[8,128]{1,0:T(8,128)S(1)} %get-tuple-element.24.mid_ref.refs_3_.refs_1_, f32[16,256]{1,0:T(8,128)S(1)} %get-tuple-element.25.own_ref.refs_2_, f32[3,256,128]{2,1,0:T(8,128)S(1)} %get-tuple-element.26.refs_4_.refs_3_, ...), custom_call_target="tpu_custom_call" | custom-call | flops 20971520 | bytes 400000 | tf_op jit(solution)/shard_map/last/pallas_call | solution.py:406
  16.9 0.0 copy-start
  16.9 0.0 copy-start.1
  16.9 2.1 %collective-permute-start.3 = (f32[16,512]{1,0:T(8,128)S(1)}, f32[16,512]{1,0:T(8,128)S(1)}, u32[]{:S(2)}, u32[]{:S(2)}) collective-permute-start(f32[16,512]{1,0:T(8,128)S(1)} %last.1), channel_id=1, source_target_pairs={{0,5},{1,4},{2,7},{3,6},{4,1},{5,0},{6,3},{7,2},{8,13},{9,12},{10,... | collective-permute-start | bytes 98312 | tf_op jit(solution)/shard_map/ppermute | solution.py:374
  19.0 1.6 %collective-permute-done.3 = f32[16,512]{1,0:T(8,128)S(1)} collective-permute-done((f32[16,512]{1,0:T(8,128)S(1)}, f32[16,512]{1,0:T(8,128)S(1)}, u32[]{:S(2)}, u32[]{:S(2)}) %collective-permute-start.3) | collective-permute-done | bytes 32800 | tf_op jit(solution)/shard_map/ppermute | solution.py:374
  20.6 1.4 %collective-permute-start.4 = (f32[16,1024]{1,0:T(8,128)S(1)}, f32[16,1024]{1,0:T(8,128)S(1)}, u32[]{:S(2)}, u32[]{:S(2)}) collective-permute-start(f32[16,1024]{1,0:T(8,128)S(1)} %pad_maximum_fusion.refs_0_), channel_id=1, source_target_pairs={{0,3},{1,2},{2,1},{3,0},{4,7},{5,6},{6,5},{7,4},{8,11},{9,10},{10,... | collective-permute-start | bytes 196616 | tf_op jit(solution)/shard_map/ppermute | solution.py:374
  22.0 0.3 collective-permute-start.6
  22.3 2.3 %collective-permute-done.4.refs_0_ = f32[16,1024]{1,0:T(8,128)S(1)} collective-permute-done((f32[16,1024]{1,0:T(8,128)S(1)}, f32[16,1024]{1,0:T(8,128)S(1)}, u32[]{:S(2)}, u32[]{:S(2)}) %collective-permute-start.4) | collective-permute-done | bytes 65568 | tf_op jit(solution)/shard_map/ppermute | solution.py:374
  24.6 0.3 %collective-permute-start.5 = (f32[16,1024]{1,0:T(8,128)S(1)}, f32[16,1024]{1,0:T(8,128)S(1)}, u32[]{:S(2)}, u32[]{:S(2)}) collective-permute-start(f32[16,1024]{1,0:T(8,128)S(1)} %collective-permute-done.4.refs_0_), channel_id=1, source_target_pairs={{0,1},{1,0},{2,3},{3,2},{4,5},{5,4},{6,7},{7,6},{8,9},{9,8},{10,11... | collective-permute-start | bytes 196616 | tf_op jit(solution)/shard_map/ppermute | solution.py:374
  24.9 0.0 copy-done
  24.9 0.0 copy-done.1
  24.9 0.3 %pick.4 = (f32[8,1536]{1,0:T(8,128)S(1)}, f32[8,1536]{1,0:T(8,128)S(1)}) custom-call(f32[16,1024]{1,0:T(8,128)S(1)} %pad_maximum_fusion.refs_0_, s32[1536]{0:T(1024)S(1)} %copy-done, s32[1536]{0:T(1024)S(1)} %copy-done.1), custom_call_target="tpu_custom_call" | custom-call | flops 1572864 | bytes 400000 | tf_op jit(solution)/shard_map/pick/pallas_call | solution.py:439
  25.2 0.0 collective-permute-done.6.refs_0_
  25.2 0.3 %pick.5 = (f32[8,1536]{1,0:T(8,128)S(1)}, f32[8,1536]{1,0:T(8,128)S(1)}) custom-call(f32[16,1024]{1,0:T(8,128)S(1)} %collective-permute-done.6.refs_0_, s32[1536]{0:T(1024)S(1)} %copy-done, s32[1536]{0:T(1024)S(1)} %copy-done.1, f32[8,1536]{1,0:T(8,128)S(1)} %get-tuple-element.38.refs_3_, f32[8,1536]{1,0:T(8,128)S(1)} %get-tuple-element.39.refs_4_), custom_call_target="tpu_custom_call" | custom-call | flops 1572864 | bytes 400000 | tf_op jit(solution)/shard_map/pick/pallas_call | solution.py:439
  25.5 0.3 %pick.6 = (f32[8,1536]{1,0:T(8,128)S(1)}, f32[8,1536]{1,0:T(8,128)S(1)}) custom-call(f32[16,1024]{1,0:T(8,128)S(1)} %collective-permute-done.4.refs_0_, s32[1536]{0:T(1024)S(1)} %copy-done, s32[1536]{0:T(1024)S(1)} %copy-done.1, f32[8,1536]{1,0:T(8,128)S(1)} %get-tuple-element.40.refs_3_, f32[8,1536]{1,0:T(8,128)S(1)} %get-tuple-element.41.refs_4_), custom_call_target="tpu_custom_call" | custom-call | flops 1572864 | bytes 400000 | tf_op jit(solution)/shard_map/pick/pallas_call | solution.py:439
  25.8 0.0 collective-permute-done.5.refs_0_
  25.9 1.0 %pick.7 = (f32[6,1536]{1,0:T(8,128)}, f32[7,1536]{1,0:T(8,128)}) custom-call(f32[16,1024]{1,0:T(8,128)S(1)} %collective-permute-done.5.refs_0_, s32[1536]{0:T(1024)S(1)} %copy-done, s32[1536]{0:T(1024)S(1)} %copy-done.1, f32[8,1536]{1,0:T(8,128)S(1)} %get-tuple-element.42.refs_3_, f32[8,1536]{1,0:T(8,128)S(1)} %get-tuple-element.43.refs_4_), custom_call_target="tpu_custom_call" | custom-call | flops 1572864 | bytes 400000 | tf_op jit(solution)/shard_map/pick/pallas_call | solution.py:439
  (1 shorter events, 0.0 us)
Async XLA Ops:
  1.6 7.0 %collective-permute-start.2 = (f32[8,1280]{1,0:T(8,128)S(1)}, f32[8,1280]{1,0:T(8,128)S(1)}, u32[]{:S(2)}, u32[]{:S(2)}) collective-permute-start(f32[8,1280]{1,0:T(8,128)S(1)} %get-tuple-element.28), channel_id=1, source_target_pairs={{0,9},{1,8},{2,11},{3,10},{4,13},{5,12},{6,15},{7,14},{8,1},{9,0},... | collective-permute-start | bytes 122888 | tf_op jit(solution)/shard_map/ppermute | solution.py:374
  5.1 3.5 %collective-permute-start.1 = (f32[8,1024]{1,0:T(8,128)S(1)}, f32[8,1024]{1,0:T(8,128)S(1)}, u32[]{:S(2)}, u32[]{:S(2)}) collective-permute-start(f32[8,1024]{1,0:T(8,128)S(1)} %get-tuple-element.23.src_ref.refs_2_), channel_id=1, source_target_pairs={{0,5},{1,4},{2,7},{3,6},{4,1},{5,0},{6,3},{7,2},{8,13},{9,12},{10,... | collective-permute-start | bytes 98312 | tf_op jit(solution)/shard_map/ppermute | solution.py:374
  7.0 7.3 %collective-permute-start = (f32[8,1024]{1,0:T(8,128)S(1)}, f32[8,1024]{1,0:T(8,128)S(1)}, u32[]{:S(2)}, u32[]{:S(2)}) collective-permute-start(f32[8,1024]{1,0:T(8,128)S(1)} %get-tuple-element.23.src_ref.refs_2_), channel_id=1, source_target_pairs={{0,13},{1,12},{2,15},{3,14},{4,9},{5,8},{6,11},{7,10},{8,5},{9,4},... | collective-permute-start | bytes 98312 | tf_op jit(solution)/shard_map/ppermute | solution.py:374
  16.9 7.9 %copy-start = (s32[1536]{0:T(1024)S(1)}, s32[1536]{0:T(1024)}, u32[]{:S(2)}) copy-start(s32[1536]{0:T(1024)} %refs_1_.7) | copy-start | bytes 18436
  16.9 7.9 %copy-start.1 = (s32[1536]{0:T(1024)S(1)}, s32[1536]{0:T(1024)}, u32[]{:S(2)}) copy-start(s32[1536]{0:T(1024)} %refs_2_.7) | copy-start | bytes 18436
  16.9 3.7 %collective-permute-start.3 = (f32[16,512]{1,0:T(8,128)S(1)}, f32[16,512]{1,0:T(8,128)S(1)}, u32[]{:S(2)}, u32[]{:S(2)}) collective-permute-start(f32[16,512]{1,0:T(8,128)S(1)} %last.1), channel_id=1, source_target_pairs={{0,5},{1,4},{2,7},{3,6},{4,1},{5,0},{6,3},{7,2},{8,13},{9,12},{10,... | collective-permute-start | bytes 98312 | tf_op jit(solution)/shard_map/ppermute | solution.py:374
  20.6 3.9 %collective-permute-start.4 = (f32[16,1024]{1,0:T(8,128)S(1)}, f32[16,1024]{1,0:T(8,128)S(1)}, u32[]{:S(2)}, u32[]{:S(2)}) collective-permute-start(f32[16,1024]{1,0:T(8,128)S(1)} %pad_maximum_fusion.refs_0_), channel_id=1, source_target_pairs={{0,3},{1,2},{2,1},{3,0},{4,7},{5,6},{6,5},{7,4},{8,11},{9,10},{10,... | collective-permute-start | bytes 196616 | tf_op jit(solution)/shard_map/ppermute | solution.py:374
  22.0 3.2 %collective-permute-start.6 = (f32[16,1024]{1,0:T(8,128)S(1)}, f32[16,1024]{1,0:T(8,128)S(1)}, u32[]{:S(2)}, u32[]{:S(2)}) collective-permute-start(f32[16,1024]{1,0:T(8,128)S(1)} %pad_maximum_fusion.refs_0_), channel_id=1, source_target_pairs={{0,1},{1,0},{2,3},{3,2},{4,5},{5,4},{6,7},{7,6},{8,9},{9,8},{10,11... | collective-permute-start | bytes 196616 | tf_op jit(solution)/shard_map/ppermute | solution.py:374
  24.6 1.3 %collective-permute-start.5 = (f32[16,1024]{1,0:T(8,128)S(1)}, f32[16,1024]{1,0:T(8,128)S(1)}, u32[]{:S(2)}, u32[]{:S(2)}) collective-permute-start(f32[16,1024]{1,0:T(8,128)S(1)} %collective-permute-done.4.refs_0_), channel_id=1, source_target_pairs={{0,1},{1,0},{2,3},{3,2},{4,5},{5,4},{6,7},{7,6},{8,9},{9,8},{10,11... | collective-permute-start | bytes 196616 | tf_op jit(solution)/shard_map/ppermute | solution.py:374
